TPU v7x, 32 devices: a whole 2x2x4 slice. The times are simulated.
32 devices in a mesh: parts: 2 (over y), ctx: 4 (over z), grid: 4 (over x, core).
Axes of the slice: x: 2, y: 2, z: 4, core: 2. Of those that a mesh axis runs over, the one named last changes fastest.
Arguments:
- frames_in: bfloat16 [4096, 1536], P(('parts', 'ctx'), 'grid'), parts along dimension 0, may hold values from -230 to 230
- norm1_gain: bfloat16 [1536], P('grid'), may hold values from 0.25 to 1.75
- norm1_bias: bfloat16 [1536], P('grid'), may hold values from -3 to 3
- w_query: bfloat16 [1536, 1536], P(None, 'grid'), may hold values from -0.5 to 0.5
- w_key: bfloat16 [1536, 1536], P(None, 'grid'), may hold values from -2 to 2
- w_value: bfloat16 [1536, 1536], P(None, 'grid'), may hold values from -0.15625 to 0.15625
- w_out: bfloat16 [1536, 1536], P('grid'), may hold values from -0.15625 to 0.15625
- norm2_gain: bfloat16 [1536], P('grid'), may hold values from 0.099609375 to 1.8984375
- norm2_bias: bfloat16 [1536], P('grid'), may hold values from -3 to 3
- w_glu_value: bfloat16 [1536, 1536], P(None, 'grid'), may hold values from -0.15625 to 0.15625
- w_glu_gate: bfloat16 [1536, 1536], P(None, 'grid'), may hold values from -0.15625 to 0.15625
- depth_kernel: float32 [31, 1536], P(None, 'grid'), may hold values from -1 to 1
- bn_scale: float32 [1536], P('grid'), may hold values from 0.25 to 1.75
- bn_shift: float32 [1536], P('grid'), may hold values from -3 to 3
- w_proj: bfloat16 [1536, 1536], P('grid'), may hold values from -0.3125 to 0.3125
Outputs:
- layer_out: bfloat16 [4096, 1536], P(('parts', 'ctx'), 'grid'), parts along dimension 0
There are 2 independent parts, one for each index of `parts`. A program takes and returns all parts, laid end to end along the dimension named above; an argument that names none is the same for every part. Nothing has to cross between parts.
All inputs are finite; a program needn't handle non-finite values.
Results may differ from a plain program's by a relative error of at most 0.009.
Values may be sent and summed in bfloat16 or wider, within the bound.
A program may use at most 256 MiB of HBM per device.

v0:
```python
import math

import jax
import jax.numpy as jnp
from jax import lax
from jax.sharding import PartitionSpec as P

HEAD_DIM = 64
KERNEL = 31
HALF = 15


EPSILON = 1e-05
NEG_LARGE = -1e30


def with_halo(cells, sides, width):
    for axis, dim in sides:
        count = lax.axis_size(axis)
        ends = count - 1
        head = lax.slice_in_dim(cells, 0, width, axis=dim)
        tail = lax.slice_in_dim(cells, cells.shape[dim] - width, cells.shape[dim], axis=dim)
        cells = jnp.concatenate(
            [
                lax.ppermute(tail, axis, [(i, (i + 1) % count) for i in range(ends)]),
                cells,
                lax.ppermute(head, axis, [((i + 1) % count, i) for i in range(ends)]),
            ],
            axis=dim,
        )
    return cells


def attend_block(state, query_heads, key_block, value_block):
    row_max, row_sum, weighted = state
    heads_dev = query_heads.shape[1]
    key_heads = key_block.reshape(key_block.shape[0], heads_dev, HEAD_DIM)
    value_heads = value_block.reshape(value_block.shape[0], heads_dev, HEAD_DIM)
    scores = jnp.einsum(
        "qhd,khd->hqk", query_heads, key_heads, preferred_element_type=jnp.float32
    ) * (1.0 / math.sqrt(HEAD_DIM))
    new_max = jnp.maximum(row_max, jnp.max(scores, axis=2))
    factor = jnp.exp(row_max - new_max)
    soft_weights = jnp.exp(scores - new_max[:, :, None])
    new_sum = row_sum * factor + jnp.sum(soft_weights, axis=2)
    mixed = jnp.einsum(
        "hqk,khd->qhd",
        soft_weights.astype(jnp.bfloat16),
        value_heads,
        preferred_element_type=jnp.float32,
    )
    mixed = mixed.reshape(mixed.shape[0], heads_dev * HEAD_DIM)
    weighted = weighted * jnp.repeat(jnp.transpose(factor), HEAD_DIM, axis=1) + mixed
    return (new_max, new_sum, weighted)


def attend_keys(state, query_heads, key_rows, value_rows):
    key_count = key_rows.shape[0]
    block_rows = math.gcd(key_count, 512)

    def loop_step(block_index, carried):
        key_block = lax.dynamic_slice_in_dim(key_rows, block_index * block_rows, block_rows, 0)
        value_block = lax.dynamic_slice_in_dim(value_rows, block_index * block_rows, block_rows, 0)
        return attend_block(carried, query_heads, key_block, value_block)

    return lax.fori_loop(0, key_count // block_rows, loop_step, state)


def project_normed(local_shard, gain_shard, shift_shard, weights):
    values = local_shard.astype(jnp.float32)
    full_width = values.shape[1] * lax.axis_size("grid")
    totals = lax.psum((jnp.sum(values, axis=1), jnp.sum(values * values, axis=1)), "grid")
    row_mean = totals[0] / full_width
    variance = totals[1] / full_width - row_mean * row_mean
    scaled = (values - row_mean[:, None]) * lax.rsqrt(variance + EPSILON)[:, None]
    normed = (scaled * gain_shard.astype(jnp.float32) + shift_shard.astype(jnp.float32)).astype(
        jnp.bfloat16
    )
    block_piece = lax.all_gather(normed, "grid", axis=1, tiled=True)
    return tuple(
        (jnp.dot(block_piece, weight, preferred_element_type=jnp.float32) for weight in weights)
    )


def branch_sum(activation, weight_rows):
    share = lax.psum_scatter(
        lax.dot_general(
            weight_rows, activation, (((0,), (1,)), ((), ())), preferred_element_type=jnp.float32
        ).astype(jnp.bfloat16),
        "grid",
        scatter_dimension=0,
        tiled=True,
    ).astype(jnp.float32)
    return jnp.transpose(share)


def on_device(
    frames_in,
    norm1_gain,
    norm1_bias,
    w_query,
    w_key,
    w_value,
    w_out,
    norm2_gain,
    norm2_bias,
    w_glu_value,
    w_glu_gate,
    depth_kernel,
    bn_scale,
    bn_shift,
    w_proj,
):
    local_frames = frames_in.shape[0]
    heads_dev = w_query.shape[1] // HEAD_DIM
    head_width = heads_dev * HEAD_DIM
    query_full, key_full, value_full = project_normed(
        frames_in, norm1_gain, norm1_bias, (w_query, w_key, w_value)
    )
    query_rows = query_full.astype(jnp.bfloat16)
    key_rows = key_full.astype(jnp.bfloat16)
    value_rows = value_full.astype(jnp.bfloat16)
    query_heads = query_rows.reshape(local_frames, heads_dev, HEAD_DIM)
    start_state = (
        jnp.full((heads_dev, local_frames), NEG_LARGE, jnp.float32),
        jnp.zeros((heads_dev, local_frames), jnp.float32),
        jnp.zeros((local_frames, head_width), jnp.float32),
    )
    final_max, final_sum, weighted = attend_keys(
        start_state,
        query_heads,
        lax.all_gather(key_rows, "ctx", axis=0, tiled=True),
        lax.all_gather(value_rows, "ctx", axis=0, tiled=True),
    )
    attended = (weighted / jnp.repeat(jnp.transpose(final_sum), HEAD_DIM, axis=1)).astype(
        jnp.bfloat16
    )
    middle = (frames_in.astype(jnp.float32) + branch_sum(attended, w_out)).astype(jnp.bfloat16)
    value_part, gate_part = project_normed(
        middle, norm2_gain, norm2_bias, (w_glu_value, w_glu_gate)
    )
    gated = (value_part * jax.nn.sigmoid(gate_part)).astype(jnp.bfloat16)
    padded = with_halo(gated, (("ctx", 0),), HALF)
    convolved = jnp.zeros((local_frames, gated.shape[1]), jnp.float32)
    for tap_index in range(KERNEL):
        convolved = convolved + depth_kernel[tap_index] * padded[
            tap_index : tap_index + local_frames
        ].astype(jnp.float32)
    activated = jax.nn.silu(convolved * bn_scale + bn_shift).astype(jnp.bfloat16)
    return (middle.astype(jnp.float32) + branch_sum(activated, w_proj)).astype(jnp.bfloat16)


def solution(mesh):
    return jax.shard_map(
        on_device,
        mesh=mesh,
        in_specs=(
            P(("parts", "ctx"), "grid"),
            P("grid"),
            P("grid"),
            P(None, "grid"),
            P(None, "grid"),
            P(None, "grid"),
            P("grid", None),
            P("grid"),
            P("grid"),
            P(None, "grid"),
            P(None, "grid"),
            P(None, "grid"),
            P("grid"),
            P("grid"),
            P("grid", None),
        ),
        out_specs=P(("parts", "ctx"), "grid"),
        check_vma=False,
    )
```

profile of v0, /device:TPU:1, one launch (start us, length us, event | category | flops | bytes accessed | tf_op | source)
XLA Modules:
  0.0 289.5 jit_solution(2642509837750959536)
XLA Ops:
  8.0 1.2 convert_reduce_fusion.1
  9.2 6.4 %all-reduce.1 = (f32[512]{0:T(512)S(1)}, f32[512]{0:T(512)S(1)}) all-reduce(f32[512]{0:T(512)S(1)} %get-tuple-element.173, f32[512]{0:T(512)S(1)} %get-tuple-element.172), channel_id=1, replica_groups=mesh['parts'=2,'ctx'=4,'grid'=4] {'grid'}, use_global_device_ids=true, to_apply=%region_3.0 | all-reduce | flops 1024 | bytes 8192 | tf_op jit(solution)/shard_map/psum | solution.py:72
  15.6 2.0 fusion.19
  17.7 21.8 %all-gather.5.cloned.1.call-done = bf16[512,1536]{1,0:T(8,128)(2,1)} async-done(((bf16[512,384]{1,0:T(8,128)(2,1)}), bf16[512,1536]{1,0:T(8,128)(2,1)}) %all-gather.5.cloned.1.call-update) | async-done | bytes 1572880 | tf_op jit(solution)/shard_map/all_gather | solution.py:79
  39.5 3.6 %convolution_convert_fusion.4 = bf16[512,384]{1,0:T(8,128)(2,1)} fusion(bf16[512,1536]{1,0:T(8,128)(2,1)} %all-gather.5.cloned.1.call-done, bf16[1536,384]{1,0:T(8,128)(2,1)} %param.21), kind=kOutput, calls=%fused_computation.66 | convolution fusion | flops 604176384 | bytes 3145728 | tf_op jit(solution)/shard_map/dot_general | solution.py:81
  43.1 3.0 %convolution_convert_fusion.2 = bf16[512,384]{1,0:T(8,128)(2,1)} fusion(bf16[512,1536]{1,0:T(8,128)(2,1)S(1)} %copy-done.7, bf16[1536,384]{1,0:T(8,128)(2,1)} %param.22), kind=kOutput, calls=%fused_computation.64 | convolution fusion | flops 604176384 | bytes 3145728 | tf_op jit(solution)/shard_map/dot_general | solution.py:81
  46.2 2.6 convolution_convert_fusion.3
  48.8 31.0 %all-gather.7.cloned.1.call-done = bf16[2048,384]{1,0:T(8,128)(2,1)} async-done(((bf16[512,384]{1,0:T(8,128)(2,1)}), bf16[2048,384]{1,0:T(8,128)(2,1)}) %all-gather.7.cloned.1.call-update) | async-done | bytes 1572880 | tf_op jit(solution)/shard_map/all_gather | solution.py:132
  79.8 37.6 %all-gather.9.cloned.1.call-done = bf16[2048,384]{1,0:T(8,128)(2,1)} async-done(((bf16[512,384]{1,0:T(8,128)(2,1)}), bf16[2048,384]{1,0:T(8,128)(2,1)}) %all-gather.9.cloned.1.call-update) | async-done | bytes 1572880 | tf_op jit(solution)/shard_map/all_gather | solution.py:133
  117.4 53.8 %while.18 = (s32[]{:T(128)}, f32[6,512]{1,0:T(8,128)S(1)}, f32[6,512]{1,0:T(8,128)}, f32[512,384]{0,1:T(8,128)S(1)}, bf16[2048,384]{1,0:T(8,128)(2,1)}, /*index=...) while((s32[]{:T(128)}, f32[6,512]{1,0:T(8,128)S(1)}, ...), condition=%wide.region_7.0_spmd.clone, body=%wide.region_4.0_spmd.clone.sunk | while | flops 415844352 | bytes 26640616 | solution.py:66
  118.8 3.7 %bitcast_reduce_fusion.2 = (f32[6,512]{1,0:T(8,128)S(1)}, f32[6,512,512]{2,1,0:T(8,128)}) fusion(bf16[512,6,64]{0,2,1:T(8,128)(2,1)S(1)} %bitcast.78, bf16[512,6,64]{0,2,1:T(8,128)(2,1)S(1)} %get-tuple-element.318), kind=kOutput, calls=%fused_computation.1.clone.1 | convolution fusion | flops 204469248 | bytes 7090176 | tf_op jit(solution)/shard_map/while/body/eval_jaxpr/qhd,khd->hqk/dot_general | solution.py:39
  122.5 3.8 %fusion.90 = f32[6,512]{1,0:T(8,128)S(1)} fusion(f32[6,512,512]{2,1,0:T(8,128)} %get-tuple-element.288, f32[6,512]{1,0:T(8,128)S(1)} %get-tuple-element.314), kind=kLoop, calls=%fused_computation.4.clone.1 | loop fusion | flops 4715520 | bytes 6316032 | tf_op jit(solution)/shard_map/while/body/eval_jaxpr/reduce_sum | solution.py:45
  126.6 4.0 %fusion.92 = f32[6,64,512]{2,1,0:T(8,128)S(1)} fusion(bf16[512,6,64]{0,2,1:T(8,128)(2,1)S(1)} %bitcast.77, f32[6,512,512]{2,1,0:T(8,128)} %get-tuple-element.288, f32[6,512]{1,0:T(8,128)S(1)} %get-tuple-element.314), kind=kOutput, calls=%fused_computation.5.clone.1 | convolution fusion | flops 206045184 | bytes 7483392 | tf_op jit(solution)/shard_map/while/body/eval_jaxpr/hqk,khd->qhd/dot_general | solution.py:46
  132.2 3.7 %bitcast_reduce_fusion.2 = (f32[6,512]{1,0:T(8,128)S(1)}, f32[6,512,512]{2,1,0:T(8,128)}) fusion(bf16[512,6,64]{0,2,1:T(8,128)(2,1)S(1)} %bitcast.78, bf16[512,6,64]{0,2,1:T(8,128)(2,1)S(1)} %get-tuple-element.318), kind=kOutput, calls=%fused_computation.1.clone.1 | convolution fusion | flops 204469248 | bytes 7090176 | tf_op jit(solution)/shard_map/while/body/eval_jaxpr/qhd,khd->hqk/dot_general | solution.py:39
  135.9 3.8 %fusion.90 = f32[6,512]{1,0:T(8,128)S(1)} fusion(f32[6,512,512]{2,1,0:T(8,128)} %get-tuple-element.288, f32[6,512]{1,0:T(8,128)S(1)} %get-tuple-element.314), kind=kLoop, calls=%fused_computation.4.clone.1 | loop fusion | flops 4715520 | bytes 6316032 | tf_op jit(solution)/shard_map/while/body/eval_jaxpr/reduce_sum | solution.py:45
  140.0 4.0 %fusion.92 = f32[6,64,512]{2,1,0:T(8,128)S(1)} fusion(bf16[512,6,64]{0,2,1:T(8,128)(2,1)S(1)} %bitcast.77, f32[6,512,512]{2,1,0:T(8,128)} %get-tuple-element.288, f32[6,512]{1,0:T(8,128)S(1)} %get-tuple-element.314), kind=kOutput, calls=%fused_computation.5.clone.1 | convolution fusion | flops 206045184 | bytes 7483392 | tf_op jit(solution)/shard_map/while/body/eval_jaxpr/hqk,khd->qhd/dot_general | solution.py:46
  145.7 3.7 %bitcast_reduce_fusion.2 = (f32[6,512]{1,0:T(8,128)S(1)}, f32[6,512,512]{2,1,0:T(8,128)}) fusion(bf16[512,6,64]{0,2,1:T(8,128)(2,1)S(1)} %bitcast.78, bf16[512,6,64]{0,2,1:T(8,128)(2,1)S(1)} %get-tuple-element.318), kind=kOutput, calls=%fused_computation.1.clone.1 | convolution fusion | flops 204469248 | bytes 7090176 | tf_op jit(solution)/shard_map/while/body/eval_jaxpr/qhd,khd->hqk/dot_general | solution.py:39
  149.4 3.8 %fusion.90 = f32[6,512]{1,0:T(8,128)S(1)} fusion(f32[6,512,512]{2,1,0:T(8,128)} %get-tuple-element.288, f32[6,512]{1,0:T(8,128)S(1)} %get-tuple-element.314), kind=kLoop, calls=%fused_computation.4.clone.1 | loop fusion | flops 4715520 | bytes 6316032 | tf_op jit(solution)/shard_map/while/body/eval_jaxpr/reduce_sum | solution.py:45
  153.5 4.0 %fusion.92 = f32[6,64,512]{2,1,0:T(8,128)S(1)} fusion(bf16[512,6,64]{0,2,1:T(8,128)(2,1)S(1)} %bitcast.77, f32[6,512,512]{2,1,0:T(8,128)} %get-tuple-element.288, f32[6,512]{1,0:T(8,128)S(1)} %get-tuple-element.314), kind=kOutput, calls=%fused_computation.5.clone.1 | convolution fusion | flops 206045184 | bytes 7483392 | tf_op jit(solution)/shard_map/while/body/eval_jaxpr/hqk,khd->qhd/dot_general | solution.py:46
  159.2 3.7 %bitcast_reduce_fusion.2 = (f32[6,512]{1,0:T(8,128)S(1)}, f32[6,512,512]{2,1,0:T(8,128)}) fusion(bf16[512,6,64]{0,2,1:T(8,128)(2,1)S(1)} %bitcast.78, bf16[512,6,64]{0,2,1:T(8,128)(2,1)S(1)} %get-tuple-element.318), kind=kOutput, calls=%fused_computation.1.clone.1 | convolution fusion | flops 204469248 | bytes 7090176 | tf_op jit(solution)/shard_map/while/body/eval_jaxpr/qhd,khd->hqk/dot_general | solution.py:39
  162.9 3.8 %fusion.90 = f32[6,512]{1,0:T(8,128)S(1)} fusion(f32[6,512,512]{2,1,0:T(8,128)} %get-tuple-element.288, f32[6,512]{1,0:T(8,128)S(1)} %get-tuple-element.314), kind=kLoop, calls=%fused_computation.4.clone.1 | loop fusion | flops 4715520 | bytes 6316032 | tf_op jit(solution)/shard_map/while/body/eval_jaxpr/reduce_sum | solution.py:45
  166.9 4.0 %fusion.92 = f32[6,64,512]{2,1,0:T(8,128)S(1)} fusion(bf16[512,6,64]{0,2,1:T(8,128)(2,1)S(1)} %bitcast.77, f32[6,512,512]{2,1,0:T(8,128)} %get-tuple-element.288, f32[6,512]{1,0:T(8,128)S(1)} %get-tuple-element.314), kind=kOutput, calls=%fused_computation.5.clone.1 | convolution fusion | flops 206045184 | bytes 7483392 | tf_op jit(solution)/shard_map/while/body/eval_jaxpr/hqk,khd->qhd/dot_general | solution.py:46
  173.0 1.6 copy.23
  175.3 26.6 %reduce-scatter.7.cloned.1.call-done = bf16[384,512]{1,0:T(8,128)(2,1)} async-done(((bf16[1536,512]{1,0:T(8,128)(2,1)}), bf16[384,512]{1,0:T(8,128)(2,1)}) %reduce-scatter.7.cloned.1.call-update) | async-done | bytes 393232
  203.4 5.7 %all-reduce = (f32[512]{0:T(512)S(1)}, f32[512]{0:T(512)S(1)}) all-reduce(f32[512]{0:T(512)S(1)} %get-tuple-element.171, f32[512]{0:T(512)S(1)} %get-tuple-element.170), channel_id=1, replica_groups=mesh['parts'=2,'ctx'=4,'grid'=4] {'grid'}, use_global_device_ids=true, to_apply=%region_12.0 | all-reduce | flops 1024 | bytes 8192 | tf_op jit(solution)/shard_map/psum | solution.py:72
  210.3 21.2 %all-gather.11.cloned.1.call-done = bf16[512,1536]{1,0:T(8,128)(2,1)} async-done(((bf16[512,384]{1,0:T(8,128)(2,1)}), bf16[512,1536]{1,0:T(8,128)(2,1)}) %all-gather.11.cloned.1.call-update) | async-done | bytes 1572880 | tf_op jit(solution)/shard_map/all_gather | solution.py:79
  231.5 2.9 %fusion.14 = f32[512,384]{1,0:T(8,128)S(1)} fusion(bf16[512,1536]{1,0:T(8,128)(2,1)} %all-gather.11.cloned.1.call-done, bf16[1536,384]{1,0:T(8,128)(2,1)} %param.27), kind=kOutput, calls=%fused_computation.62 | convolution fusion | flops 604569600 | bytes 3538944 | tf_op jit(solution)/shard_map/dot_general | solution.py:81
  235.5 1.3 collective-permute-start.1
  236.8 4.2 %collective-permute-start = (bf16[15,384]{1,0:T(8,128)(2,1)S(1)}, bf16[15,384]{1,0:T(8,128)(2,1)S(1)}, u32[]{:S(2)}, u32[]{:S(2)}) collective-permute-start(bf16[15,384]{1,0:T(8,128)(2,1)S(1)} %get-tuple-element.230), channel_id=1, source_target_pairs={{0,4},{4,8},{8,12},{1,5},{5,9},{9,13},{2,6},{6,10},{10,14},{3,7},{... | collective-permute-start | bytes 34568 | tf_op jit(solution)/shard_map/ppermute | solution.py:25
  241.6 7.4 %fusion.11 = bf16[1536,512]{0,1:T(8,128)(2,1)S(1)} fusion(bf16[384,1536]{1,0:T(8,128)(2,1)S(1)} %copy-done.10, bf16[512,384]{1,0:T(8,128)(2,1)S(1)} %fusion.15, bf16[15,384]{1,0:T(8,128)(2,1)S(1)} %collective-permute-done.1, bf16[15,384]{1,0:T(8,128)(2,1)S(1)} %collective-permute-done, f32[384]{0:T(512)S(1)} %copy-done.11, f32[384]{0:T(512)S(1)} %copy-done.12, ...), kind=kOutput, calls=%fused_computation.21 | convolution fusion | flops 641925120 | bytes 3219456 | tf_op jit(solution)/shard_map/dot_general | solution.py:87
  249.0 1.6 copy.25
  250.6 30.0 %reduce-scatter.9.cloned.1.call-done = bf16[384,512]{1,0:T(8,128)(2,1)} async-done(((bf16[1536,512]{1,0:T(8,128)(2,1)}), bf16[384,512]{1,0:T(8,128)(2,1)}) %reduce-scatter.9.cloned.1.call-update) | async-done | bytes 393232
  (100 shorter events, 17.9 us)
Async XLA Ops:
  6.5 165.5 %copy-start = (bf16[384,1536]{1,0:T(8,128)(2,1)S(1)}, bf16[384,1536]{1,0:T(8,128)(2,1)}, u32[]{:S(2)}) copy-start(bf16[384,1536]{1,0:T(8,128)(2,1)} %param.23) | copy-start | bytes 3538948
  6.5 32.9 %all-gather.5.cloned.1.call-start = ((), (), s32[]{:S(2)}) async-start(), calls=%async_computation.2 | async-start | bytes 1966080 | tf_op jit(solution)/shard_map/all_gather | solution.py:79
  17.6 62.2 %all-gather.7.cloned.1.call-start = ((), (), s32[]{:S(2)}) async-start(), calls=%async_computation.3 | async-start | bytes 1966080 | tf_op jit(solution)/shard_map/all_gather | solution.py:132
  39.5 3.7 %copy-start.7 = (bf16[512,1536]{1,0:T(8,128)(2,1)S(1)}, bf16[512,1536]{1,0:T(8,128)(2,1)}, u32[]{:S(2)}) copy-start(bf16[512,1536]{1,0:T(8,128)(2,1)} %all-gather.5.cloned.1.call-done) | copy-start | bytes 4718596
  43.1 74.3 %all-gather.9.cloned.1.call-start = ((), (), s32[]{:S(2)}) async-start(), calls=%async_computation.4 | async-start | bytes 1966080 | tf_op jit(solution)/shard_map/all_gather | solution.py:133
  46.1 155.8 %reduce-scatter.7.cloned.1.call-start = ((), (), s32[]{:S(2)}) async-start(), calls=%async_computation.6 | async-start | bytes 1966080
  122.5 3.8 %copy-start.2 = (f32[6,512]{1,0:T(8,128)S(1)}, f32[6,512]{1,0:T(8,128)}, u32[]{:S(2)}) copy-start(f32[6,512]{1,0:T(8,128)} %get-tuple-element.304) | copy-start | bytes 36868 | tf_op jit(solution)/shard_map/while
  126.4 4.5 %copy-start.3 = (f32[6,512]{1,0:T(8,128)}, f32[6,512]{1,0:T(8,128)S(1)}, u32[]{:S(2)}) copy-start(f32[6,512]{1,0:T(8,128)S(1)} %fusion.91) | copy-start | bytes 36868 | tf_op jit(solution)/shard_map/while
  135.9 3.8 %copy-start.2 = (f32[6,512]{1,0:T(8,128)S(1)}, f32[6,512]{1,0:T(8,128)}, u32[]{:S(2)}) copy-start(f32[6,512]{1,0:T(8,128)} %get-tuple-element.304) | copy-start | bytes 36868 | tf_op jit(solution)/shard_map/while
  139.8 4.5 %copy-start.3 = (f32[6,512]{1,0:T(8,128)}, f32[6,512]{1,0:T(8,128)S(1)}, u32[]{:S(2)}) copy-start(f32[6,512]{1,0:T(8,128)S(1)} %fusion.91) | copy-start | bytes 36868 | tf_op jit(solution)/shard_map/while
  149.4 3.8 %copy-start.2 = (f32[6,512]{1,0:T(8,128)S(1)}, f32[6,512]{1,0:T(8,128)}, u32[]{:S(2)}) copy-start(f32[6,512]{1,0:T(8,128)} %get-tuple-element.304) | copy-start | bytes 36868 | tf_op jit(solution)/shard_map/while
  153.3 4.5 %copy-start.3 = (f32[6,512]{1,0:T(8,128)}, f32[6,512]{1,0:T(8,128)S(1)}, u32[]{:S(2)}) copy-start(f32[6,512]{1,0:T(8,128)S(1)} %fusion.91) | copy-start | bytes 36868 | tf_op jit(solution)/shard_map/while
  162.9 3.8 %copy-start.2 = (f32[6,512]{1,0:T(8,128)S(1)}, f32[6,512]{1,0:T(8,128)}, u32[]{:S(2)}) copy-start(f32[6,512]{1,0:T(8,128)} %get-tuple-element.304) | copy-start | bytes 36868 | tf_op jit(solution)/shard_map/while
  166.7 4.5 %copy-start.3 = (f32[6,512]{1,0:T(8,128)}, f32[6,512]{1,0:T(8,128)S(1)}, u32[]{:S(2)}) copy-start(f32[6,512]{1,0:T(8,128)S(1)} %fusion.91) | copy-start | bytes 36868 | tf_op jit(solution)/shard_map/while
  174.6 0.7 copy-start.5
  174.6 0.7 copy-start.6
  174.6 28.5 %copy-start.1 = (bf16[512,384]{1,0:T(8,128)(2,1)S(1)}, bf16[512,384]{1,0:T(8,128)(2,1)}, u32[]{:S(2)}) copy-start(bf16[512,384]{1,0:T(8,128)(2,1)} %param.17) | copy-start | bytes 1179652
  174.7 56.8 %all-gather.11.cloned.1.call-start = ((), (), s32[]{:S(2)}) async-start(), calls=%async_computation.5 | async-start | bytes 1966080 | tf_op jit(solution)/shard_map/all_gather | solution.py:79
  175.3 34.9 %copy-start.4 = (f32[31,384]{1,0:T(8,128)S(1)}, f32[31,384]{1,0:T(8,128)}, u32[]{:S(2)}) copy-start(f32[31,384]{1,0:T(8,128)} %param.28) | copy-start | bytes 142852
  210.2 70.4 %reduce-scatter.9.cloned.1.call-start = ((), (), s32[]{:S(2)}) async-start(), calls=%async_computation.7 | async-start | bytes 1966080
  231.5 3.0 %copy-start.8 = (bf16[512,1536]{1,0:T(8,128)(2,1)S(1)}, bf16[512,1536]{1,0:T(8,128)(2,1)}, u32[]{:S(2)}) copy-start(bf16[512,1536]{1,0:T(8,128)(2,1)} %all-gather.11.cloned.1.call-done) | copy-start | bytes 4718596
  231.5 3.0 %copy-start.9 = (bf16[1536,384]{1,0:T(8,128)(2,1)S(1)}, bf16[1536,384]{1,0:T(8,128)(2,1)}, u32[]{:S(2)}) copy-start(bf16[1536,384]{1,0:T(8,128)(2,1)} %param.26) | copy-start | bytes 3538948
  234.5 7.1 %copy-start.10 = (bf16[384,1536]{1,0:T(8,128)(2,1)S(1)}, bf16[384,1536]{1,0:T(8,128)(2,1)}, u32[]{:S(2)}) copy-start(bf16[384,1536]{1,0:T(8,128)(2,1)} %param.31) | copy-start | bytes 3538948
  234.5 7.1 %copy-start.11 = (f32[384]{0:T(512)S(1)}, f32[384]{0:T(512)}, u32[]{:S(2)}) copy-start(f32[384]{0:T(512)} %param.30) | copy-start | bytes 4612
  234.5 7.1 %copy-start.12 = (f32[384]{0:T(512)S(1)}, f32[384]{0:T(512)}, u32[]{:S(2)}) copy-start(f32[384]{0:T(512)} %param.29) | copy-start | bytes 4612
  235.5 5.5 %collective-permute-start.1 = (bf16[15,384]{1,0:T(8,128)(2,1)S(1)}, bf16[15,384]{1,0:T(8,128)(2,1)S(1)}, u32[]{:S(2)}, u32[]{:S(2)}) collective-permute-start(bf16[15,384]{1,0:T(8,128)(2,1)S(1)} %get-tuple-element.231), channel_id=1, source_target_pairs={{4,0},{8,4},{12,8},{5,1},{9,5},{13,9},{6,2},{10,6},{14,10},{7,3},{... | collective-permute-start | bytes 34568 | tf_op jit(solution)/shard_map/ppermute | solution.py:27
  236.8 4.8 %collective-permute-start = (bf16[15,384]{1,0:T(8,128)(2,1)S(1)}, bf16[15,384]{1,0:T(8,128)(2,1)S(1)}, u32[]{:S(2)}, u32[]{:S(2)}) collective-permute-start(bf16[15,384]{1,0:T(8,128)(2,1)S(1)} %get-tuple-element.230), channel_id=1, source_target_pairs={{0,4},{4,8},{8,12},{1,5},{5,9},{9,13},{2,6},{6,10},{10,14},{3,7},{... | collective-permute-start | bytes 34568 | tf_op jit(solution)/shard_map/ppermute | solution.py:25
Sparse Core Ops, SparseCore 0:
  17.7 21.6 all-gather.4
  43.2 36.5 all-gather.6
  81.4 35.9 all-gather.8
  174.8 27.1 reduce-scatter.6
  210.3 21.1 all-gather.10
  250.7 29.8 reduce-scatter.8
where the time goes:
time: 291 us; the launch traced here: 290 us
  waiting for transfers between devices  169 us (58%)
  matrix products  52.1 us (18%)
  other arithmetic  24 us (8%)
  between operations  13.7 us (5%)
  local copies, waits for them, and re-layouts  12.8 us (4%)
  blocking collectives  12.1 us (4%)
  starting transfers between devices  5.67 us (2%)
    unnamed x8, waiting for transfers between devices  56.7 us
    all_gather x2, waiting for transfers between devices, project_normed(): block_piece = lax.all_gather(normed, 'grid', axis=1, tiled=True)  43 us
    all_gather x1, waiting for transfers between devices, on_device(): lax.all_gather(value_rows, 'ctx', axis=0, tiled=True)  37.6 us
    all_gather x1, waiting for transfers between devices, on_device(): lax.all_gather(key_rows, 'ctx', axis=0, tiled=True)  31 us
    dot_general x4, matrix products, attend_block(): jnp.einsum('hqk,khd->qhd', soft_weights.astype(jnp.bfloat16), value_heads...  15.9 us
    reduce_sum x4, other arithmetic, attend_block(): new_sum = row_sum * factor + jnp.sum(soft_weights, axis=2)  15.3 us
    dot_general x4, matrix products, attend_block(): jnp.einsum('qhd,khd->hqk', query_heads, key_heads, preferred_element_type...  14.8 us
    dot_general x5, matrix products, project_normed(): jnp.dot(block_piece, weight, preferred_element_type=jnp.float32)  13.1 us
  transfers between devices with their start and end apart: 8, of which 7 were waited for; matrix products, arithmetic and copies ran while one was open for 2% of the time, Pallas kernels for 0%

commit v1 on v0

v1 whole, which is shorter than its diff:
```python
import math

import jax
import jax.numpy as jnp
from jax import lax
from jax.experimental import pallas as pl
from jax.experimental.pallas import tpu as pltpu
from jax.sharding import PartitionSpec as P

HEAD_DIM = 64
KERNEL = 31
HALF = 15
EPSILON = 1e-05
LANES = 128
PAD = 16
MESH = pl.DeviceIdType.MESH
F32 = jnp.float32
BF16 = jnp.bfloat16
VMEM_LIMIT = 56 * 1024 * 1024


def remote(src, dst, send, recv, axis, index):
    return pltpu.make_async_remote_copy(
        src_ref=src,
        dst_ref=dst,
        send_sem=send,
        recv_sem=recv,
        device_id={axis: index},
        device_id_type=MESH,
    )


class GridGather:
    def __init__(self, size, sems):
        self.me = lax.axis_index("grid")
        self.chips = size // 2
        self.chip = self.me // 2
        self.core = self.me % 2
        self.mate = self.chip * 2 + 1 - self.core
        self.sems = sems

    def peer(self, step):
        return lax.rem(self.chip + step, self.chips) * 2 + self.core

    def source(self, step):
        return lax.rem(self.chip + self.chips - step, self.chips) * 2 + self.core

    def source_mate(self, step):
        return lax.rem(self.chip + self.chips - step, self.chips) * 2 + 1 - self.core

    def greet(self, barrier):
        pl.semaphore_signal(barrier, inc=1, device_id={"grid": self.mate}, device_id_type=MESH)
        for step in range(1, self.chips):
            pl.semaphore_signal(
                barrier, inc=1, device_id={"grid": self.peer(step)}, device_id_type=MESH
            )
        return self.chips

    def own(self, view, part, step):
        ref = view(self.me)
        target = self.mate if step == 0 else self.peer(step)
        return remote(ref, ref, self.sems.at[0, step, part], self.sems.at[1, step, part], "grid", target)

    def arrived(self, view, part, step):
        slot = self.mate if step == 0 else self.source(step)
        ref = view(slot)
        return remote(ref, ref, self.sems.at[0, step, part], self.sems.at[1, step, part], "grid", self.mate)

    def relay(self, view, part, step):
        ref = view(self.source(step))
        return remote(ref, ref, self.sems.at[2, step, part], self.sems.at[3, step, part], "grid", self.mate)

    def relayed(self, view, part, step):
        ref = view(self.source_mate(step))
        return remote(ref, ref, self.sems.at[2, step, part], self.sems.at[3, step, part], "grid", self.mate)

    def start(self, view, part):
        for step in range(1, self.chips):
            self.own(view, part, step).start()
        self.own(view, part, 0).start()

    def forward(self, view, part):
        for step in range(1, self.chips):
            self.arrived(view, part, step).wait_recv()
            self.relay(view, part, step).start()

    def finish(self, view, part):
        self.arrived(view, part, 0).wait_recv()
        for step in range(1, self.chips):
            self.relayed(view, part, step).wait_recv()

    def drain(self, view, part):
        for step in range(self.chips):
            self.own(view, part, step).wait_send()
        for step in range(1, self.chips):
            self.relay(view, part, step).wait_send()


def gather_sems(size, parts):
    return pltpu.SemaphoreType.DMA((4, size // 2, parts))


def normalize(pieces, gains, shifts):
    width = pieces[0].shape[1] * len(pieces)
    total = sum(jnp.sum(piece, axis=1, keepdims=True) for piece in pieces)
    mean = total / width
    centred = [piece - mean for piece in pieces]
    square = sum(jnp.sum(piece * piece, axis=1, keepdims=True) for piece in centred)
    scale = lax.rsqrt(square / width + EPSILON)
    return [
        (piece * scale * gain + shift).astype(BF16)
        for piece, gain, shift in zip(centred, gains, shifts)
    ]


def project(pieces, weight_ref):
    width = pieces[0].shape[1]
    total = None
    for index, piece in enumerate(pieces):
        term = jnp.dot(
            piece, weight_ref[index * width : (index + 1) * width, :], preferred_element_type=F32
        )
        total = term if total is None else total + term
    return total


def first_kernel(
    size, parts, x_ref, affine_ref, wq_hbm, wk_hbm, wv_hbm,
    xg_ref, affg_ref, q_ref, kv_ref,
    wq_ref, wk_ref, wv_ref, sems, aff_sems, load_sems,
):
    rows = x_ref.shape[0]
    step_rows = rows // parts
    gather = GridGather(size, sems)
    small = GridGather(size, aff_sems)
    loads = [
        pltpu.make_async_copy(src, dst, load_sems.at[index])
        for index, (src, dst) in enumerate(((wq_hbm, wq_ref), (wk_hbm, wk_ref), (wv_hbm, wv_ref)))
    ]
    for load in loads:
        load.start()
    barrier = pltpu.get_barrier_semaphore()
    count = gather.greet(barrier)
    xg_ref[gather.me] = x_ref[...]
    affg_ref[gather.me] = affine_ref[...]
    pl.semaphore_wait(barrier, count)

    def view(part):
        return lambda slot: xg_ref.at[slot, pl.ds(part * step_rows, step_rows), :]

    def small_view(slot):
        return affg_ref.at[slot]

    small.start(small_view, 0)
    for part in range(parts):
        gather.start(view(part), part)
    small.forward(small_view, 0)
    gather.forward(view(0), 0)
    small.finish(small_view, 0)
    for load in loads:
        load.wait()
    gains = [affg_ref[index, 0:1, :] for index in range(size)]
    shifts = [affg_ref[index, 1:2, :] for index in range(size)]
    scale = math.log2(math.e) / math.sqrt(HEAD_DIM)
    for part in range(parts):
        if part + 1 < parts:
            gather.forward(view(part + 1), part + 1)
        gather.finish(view(part), part)
        span = slice(part * step_rows, (part + 1) * step_rows)
        pieces = [xg_ref[index, span, :].astype(F32) for index in range(size)]
        normed = normalize(pieces, gains, shifts)
        q_ref[span, :] = (project(normed, wq_ref) * scale).astype(BF16)
        kv_ref[0, span, :] = project(normed, wk_ref).astype(BF16)
        kv_ref[1, span, :] = project(normed, wv_ref).astype(BF16)
    small.drain(small_view, 0)
    for part in range(parts):
        gather.drain(view(part), part)


def attend_kernel(
    size, count, parts, q_ref, kv_ref, wo_ref, wp_ref,
    att_ref, wog_ref, wpg_ref,
    kvg_ref, qm_ref, max_ref, acc_ref, right_sems, left_sems, wo_sems, wp_sems, load_sems,
):
    rows, width = q_ref.shape
    heads = width // HEAD_DIM
    step_rows = rows // parts
    ctx = lax.axis_index("ctx")
    gather = GridGather(size, wo_sems)
    me = gather.me
    has_left = ctx > 0
    has_right = ctx < count - 1
    barrier = pltpu.get_barrier_semaphore()
    for step in range(1, size):
        pl.semaphore_signal(
            barrier, inc=1, device_id={"grid": lax.rem(me + step, size)}, device_id_type=MESH
        )

    @pl.when(has_left)
    def _():
        pl.semaphore_signal(barrier, inc=1, device_id={"ctx": ctx - 1}, device_id_type=MESH)

    @pl.when(has_right)
    def _():
        pl.semaphore_signal(barrier, inc=1, device_id={"ctx": ctx + 1}, device_id_type=MESH)

    kvg_ref[ctx] = kv_ref[...]
    inner = (ctx + count - 1) // count + (2 * count - 2 - ctx) // count
    pl.semaphore_wait(barrier, size - 1 + inner)

    def block(slot, part):
        return kvg_ref.at[slot, :, pl.ds(part * step_rows, step_rows), :]

    def to_right(step, part):
        ref = block(ctx - step, part)
        return remote(ref, ref, right_sems.at[0, step, part], right_sems.at[1, step, part], "ctx", ctx + 1)

    def from_left(step, part):
        ref = block(ctx - 1 - step, part)
        return remote(ref, ref, right_sems.at[0, step, part], right_sems.at[1, step, part], "ctx", ctx - 1)

    def to_left(step, part):
        ref = block(ctx + step, part)
        return remote(ref, ref, left_sems.at[0, step, part], left_sems.at[1, step, part], "ctx", ctx - 1)

    def from_right(step, part):
        ref = block(ctx + 1 + step, part)
        return remote(ref, ref, left_sems.at[0, step, part], left_sems.at[1, step, part], "ctx", ctx + 1)

    for part in range(parts):

        @pl.when(has_right)
        def _():
            to_right(0, part).start()

        @pl.when(has_left)
        def _():
            to_left(0, part).start()

    def wo_view(slot):
        return wog_ref.at[slot]

    for step in range(gather.chips):
        target = gather.mate if step == 0 else gather.peer(step)
        remote(wo_ref, wog_ref.at[me], wo_sems.at[0, step, 0], wo_sems.at[1, step, 0], "grid", target).start()

    def send_wp(step):
        target = lax.rem(me + step, size)
        return remote(wp_ref.at[target], wpg_ref.at[me], wp_sems.at[0, step], wp_sems.at[1, step], "grid", target)

    for step in range(1, size):
        send_wp(step).start()
    loads = [
        pltpu.make_async_copy(wo_ref, wog_ref.at[me], load_sems.at[0]),
        pltpu.make_async_copy(wp_ref.at[me], wpg_ref.at[me], load_sems.at[1]),
    ]
    for load in loads:
        load.start()

    spans = []
    for head in range(heads):
        low = head * HEAD_DIM // LANES * LANES
        high = min(low + LANES, width)
        spans.append((low, high))
        pair = q_ref[:, low:high]
        lane = lax.broadcasted_iota(jnp.int32, pair.shape, 1)
        inside = lane // HEAD_DIM == (head * HEAD_DIM - low) // HEAD_DIM
        qm_ref[head, :, 0 : high - low] = jnp.where(inside, pair, jnp.zeros_like(pair))

    def attend(slot, first):
        for head in range(heads):
            low, high = spans[head]
            keys = kvg_ref[slot, 0, :, low:high]
            values = kvg_ref[slot, 1, :, low:high]
            extra = [jnp.ones((rows, LANES), BF16)]
            if high - low < LANES:
                extra = [jnp.zeros((rows, LANES - (high - low)), BF16)] + extra
            values = jnp.concatenate([values] + extra, axis=1)
            scores = lax.dot_general(
                qm_ref[head, :, 0 : high - low], keys, (((1,), (1,)), ((), ())),
                preferred_element_type=F32,
            )
            peak = jnp.max(scores, axis=1, keepdims=True)
            if first:
                peak = jnp.broadcast_to(peak, (rows, LANES))
                soft = jnp.exp2(scores - jnp.concatenate([peak] * (rows // LANES), axis=1)).astype(BF16)
                acc_ref[head] = jnp.dot(soft, values, preferred_element_type=F32)
            else:
                old = max_ref[head]
                peak = jnp.maximum(old, peak)
                factor = jnp.exp2(old - peak)
                soft = jnp.exp2(scores - jnp.concatenate([peak] * (rows // LANES), axis=1)).astype(BF16)
                acc_ref[head] = acc_ref[head] * jnp.concatenate([factor, factor], axis=1) + jnp.dot(
                    soft, values, preferred_element_type=F32
                )
            max_ref[head] = peak

    attend(ctx, True)

    @pl.loop(0, count - 1)
    def _(step):
        left_there = ctx - 1 - step >= 0
        right_there = ctx + 1 + step <= count - 1
        for part in range(parts):

            @pl.when(left_there)
            def _():
                from_left(step, part).wait_recv()

                @pl.when(has_right)
                def _():
                    to_right(step + 1, part).start()

            @pl.when(right_there)
            def _():
                from_right(step, part).wait_recv()

                @pl.when(has_left)
                def _():
                    to_left(step + 1, part).start()

        @pl.when(step == count - 2)
        def _():
            gather.forward(wo_view, 0)

        @pl.loop(0, 2)
        def _(side):
            slot = jnp.where(side == 0, ctx - 1 - step, ctx + 1 + step)

            @pl.when((slot >= 0) & (slot <= count - 1))
            def _():
                attend(slot, False)

    for pair in range((heads + 1) // 2):
        low, high = spans[2 * pair]
        results = [
            acc_ref[head, :, 0:LANES] / acc_ref[head, :, LANES : 2 * LANES]
            for head in range(2 * pair, min(2 * pair + 2, heads))
        ]
        if len(results) == 2:
            lane = lax.broadcasted_iota(jnp.int32, (rows, LANES), 1)
            mixed = jnp.where(lane < HEAD_DIM, results[0], results[1])
        else:
            mixed = results[0]
        att_ref[:, low:high] = mixed[:, 0 : high - low].astype(BF16)

    gather.finish(wo_view, 0)
    for step in range(gather.chips):
        target = gather.mate if step == 0 else gather.peer(step)
        remote(wo_ref, wog_ref.at[me], wo_sems.at[0, step, 0], wo_sems.at[1, step, 0], "grid", target).wait_send()
    for step in range(1, gather.chips):
        gather.relay(wo_view, 0, step).wait_send()
    for step in range(1, size):
        send_wp(step).wait_send()
        source = lax.rem(me + size - step, size)
        remote(wp_ref.at[me], wpg_ref.at[source], wp_sems.at[0, step], wp_sems.at[1, step], "grid", source).wait_recv()
    for load in loads:
        load.wait()

    @pl.loop(0, count - 1)
    def _(step):
        for part in range(parts):

            @pl.when(has_right & (ctx - step >= 0))
            def _():
                to_right(step, part).wait_send()

            @pl.when(has_left & (ctx + step <= count - 1))
            def _():
                to_left(step, part).wait_send()


def last_kernel(
    size, count, parts, att_ref, xg_ref, affg_ref, wog_hbm, wgv_hbm, wgg_hbm, wpg_hbm,
    taps_ref, bn_ref, out_ref,
    attg_ref, actg_ref, mid_ref, gated_ref, wo_ref, wgv_ref, wgg_ref, wp_ref,
    att_sems, act_sems, halo_sems, load_sems,
):
    rows, width = att_ref.shape
    step_rows = rows // parts
    ctx = lax.axis_index("ctx")
    attended = GridGather(size, att_sems)
    activated = GridGather(size, act_sems)
    me = attended.me
    has_left = ctx > 0
    has_right = ctx < count - 1
    loads = [
        pltpu.make_async_copy(src, dst, load_sems.at[index])
        for index, (src, dst) in enumerate(
            ((wog_hbm, wo_ref), (wgv_hbm, wgv_ref), (wgg_hbm, wgg_ref), (wpg_hbm, wp_ref))
        )
    ]
    for load in loads:
        load.start()
    barrier = pltpu.get_barrier_semaphore()
    greeted = attended.greet(barrier)

    @pl.when(has_left)
    def _():
        pl.semaphore_signal(barrier, inc=1, device_id={"ctx": ctx - 1}, device_id_type=MESH)

    @pl.when(has_right)
    def _():
        pl.semaphore_signal(barrier, inc=1, device_id={"ctx": ctx + 1}, device_id_type=MESH)

    attg_ref[me] = att_ref[...]
    inner = (ctx + count - 1) // count + (2 * count - 2 - ctx) // count
    pl.semaphore_wait(barrier, greeted + inner)

    def view(buffer, part):
        return lambda slot: buffer.at[slot, pl.ds(part * step_rows, step_rows), :]

    for part in range(parts):
        attended.start(view(attg_ref, part), part)

    @pl.when(jnp.logical_not(has_left))
    def _():
        gated_ref[0:PAD, :] = jnp.zeros((PAD, width), F32)

    @pl.when(jnp.logical_not(has_right))
    def _():
        gated_ref[PAD + rows : 2 * PAD + rows, :] = jnp.zeros((PAD, width), F32)

    def halo_left(index):
        return remote(
            gated_ref.at[PAD : 2 * PAD, :], gated_ref.at[PAD + rows : 2 * PAD + rows, :],
            halo_sems.at[0], halo_sems.at[1], "ctx", index,
        )

    def halo_right(index):
        return remote(
            gated_ref.at[rows : rows + PAD, :], gated_ref.at[0:PAD, :],
            halo_sems.at[2], halo_sems.at[3], "ctx", index,
        )

    attended.forward(view(attg_ref, 0), 0)
    for load in loads:
        load.wait()
    gains = [affg_ref[index, 2:3, :] for index in range(size)]
    shifts = [affg_ref[index, 3:4, :] for index in range(size)]
    for part in range(parts):
        if part + 1 < parts:
            attended.forward(view(attg_ref, part + 1), part + 1)
        attended.finish(view(attg_ref, part), part)
        span = slice(part * step_rows, (part + 1) * step_rows)
        sources = [attg_ref[index, span, :] for index in range(size)]
        pieces = []
        for column in range(size):
            total = xg_ref[column, span, :].astype(F32)
            for index in range(size):
                total = total + jnp.dot(
                    sources[index], wo_ref[index, column], preferred_element_type=F32
                )
            middle = total.astype(BF16)
            mid_ref[column, span, :] = middle
            pieces.append(middle.astype(F32))
        normed = normalize(pieces, gains, shifts)
        gate = project(normed, wgg_ref)
        value = project(normed, wgv_ref)
        gated = (value * (1.0 / (1.0 + jnp.exp(-gate)))).astype(BF16)
        gated_ref[PAD + part * step_rows : PAD + (part + 1) * step_rows, :] = gated.astype(F32)
        if part == 0:

            @pl.when(has_left)
            def _():
                halo_left(ctx - 1).start()

    @pl.when(has_right)
    def _():
        halo_right(ctx + 1).start()

    block_rows = min(32, step_rows)
    inner_parts = list(range(1, parts - 1))
    for order, part in enumerate(inner_parts + [0] + ([parts - 1] if parts > 1 else [])):
        if order == len(inner_parts):

            @pl.when(has_left)
            def _():
                halo_right(ctx - 1).wait_recv()

            @pl.when(has_right)
            def _():
                halo_left(ctx + 1).wait_recv()

        @pl.loop(0, step_rows // block_rows)
        def _(block):
            base = pl.multiple_of(part * step_rows + block * block_rows, block_rows)
            window = gated_ref[pl.ds(base, block_rows + 2 * PAD), :]
            total = jnp.zeros((block_rows, width), F32)
            for tap in range(KERNEL):
                low = tap + PAD - HALF
                total = total + taps_ref[tap : tap + 1, :] * window[low : low + block_rows, :]
            scaled = total * bn_ref[0:1, :] + bn_ref[1:2, :]
            result = scaled / (1.0 + jnp.exp(-scaled))
            actg_ref[me, pl.ds(base, block_rows), :] = result.astype(BF16)

        activated.start(view(actg_ref, part), part)

    sequence = inner_parts + [0] + ([parts - 1] if parts > 1 else [])
    activated.forward(view(actg_ref, sequence[0]), sequence[0])
    for order, part in enumerate(sequence):
        if order + 1 < parts:
            activated.forward(view(actg_ref, sequence[order + 1]), sequence[order + 1])
        activated.finish(view(actg_ref, part), part)
        span = slice(part * step_rows, (part + 1) * step_rows)
        total = mid_ref[me, span, :].astype(F32)
        for index in range(size):
            total = total + jnp.dot(
                actg_ref[index, span, :], wp_ref[index], preferred_element_type=F32
            )
        out_ref[span, :] = total.astype(BF16)

    for part in range(parts):
        attended.drain(view(attg_ref, part), part)
        activated.drain(view(actg_ref, part), part)

    @pl.when(has_left)
    def _():
        halo_left(ctx - 1).wait_send()

    @pl.when(has_right)
    def _():
        halo_right(ctx + 1).wait_send()


def params(number):
    return pltpu.CompilerParams(
        collective_id=number, has_side_effects=True, vmem_limit_bytes=VMEM_LIMIT
    )


def on_device(
    frames_in,
    norm1_gain,
    norm1_bias,
    w_query,
    w_key,
    w_value,
    w_out,
    norm2_gain,
    norm2_bias,
    w_glu_value,
    w_glu_gate,
    depth_kernel,
    bn_scale,
    bn_shift,
    w_proj,
):
    size = lax.axis_size("grid")
    count = lax.axis_size("ctx")
    rows, width = frames_in.shape
    full = width * size
    heads = width // HEAD_DIM
    vmem = pl.BlockSpec(memory_space=pltpu.VMEM)
    anywhere = pl.BlockSpec(memory_space=pl.ANY)
    dma = pltpu.SemaphoreType.DMA
    parts = 4

    def shape(dims, dtype=BF16):
        return jax.ShapeDtypeStruct(dims, dtype)

    affine = jnp.stack([norm1_gain, norm1_bias, norm2_gain, norm2_bias]).astype(F32)
    affine = jnp.pad(affine, ((0, 4), (0, 0)))
    wo_blocks = jnp.transpose(w_out.reshape(width, size, width), (1, 0, 2))
    wp_blocks = jnp.transpose(w_proj.reshape(width, size, width), (1, 0, 2))

    xg, affg, queries, key_values = pl.pallas_call(
        lambda *refs: first_kernel(size, parts, *refs),
        out_shape=(
            shape((size, rows, width)),
            shape((size, 8, width), F32),
            shape((rows, width)),
            shape((2, rows, width)),
        ),
        in_specs=[vmem, vmem, anywhere, anywhere, anywhere],
        out_specs=(vmem,) * 4,
        scratch_shapes=[pltpu.VMEM((full, width), BF16)] * 3
        + [gather_sems(size, parts), gather_sems(size, 1), dma((3,))],
        compiler_params=params(0),
        name="gather_project",
    )(frames_in, affine, w_query, w_key, w_value)

    kv_parts = 2
    attended, wo_all, wp_all = pl.pallas_call(
        lambda *refs: attend_kernel(size, count, kv_parts, *refs),
        out_shape=(
            shape((rows, width)),
            shape((size, size, width, width)),
            shape((size, width, width)),
        ),
        in_specs=[vmem, vmem, anywhere, anywhere],
        out_specs=(vmem, anywhere, anywhere),
        scratch_shapes=[
            pltpu.VMEM((count, 2, rows, width), BF16),
            pltpu.VMEM((heads, rows, LANES), BF16),
            pltpu.VMEM((heads, rows, LANES), F32),
            pltpu.VMEM((heads, rows, 2 * LANES), F32),
            dma((2, count, kv_parts)),
            dma((2, count, kv_parts)),
            gather_sems(size, 1),
            dma((2, size)),
            dma((2,)),
        ],
        compiler_params=params(1),
        name="attend_ring",
    )(queries, key_values, wo_blocks, wp_blocks)

    norms = jnp.stack([bn_scale, bn_shift])
    return pl.pallas_call(
        lambda *refs: last_kernel(size, count, parts, *refs),
        out_shape=shape((rows, width)),
        in_specs=[vmem, vmem, vmem] + [anywhere] * 4 + [vmem, vmem],
        out_specs=vmem,
        scratch_shapes=[
            pltpu.VMEM((size, rows, width), BF16),
            pltpu.VMEM((size, rows, width), BF16),
            pltpu.VMEM((size, rows, width), BF16),
            pltpu.VMEM((rows + 2 * PAD, width), F32),
            pltpu.VMEM((size, size, width, width), BF16),
            pltpu.VMEM((full, width), BF16),
            pltpu.VMEM((full, width), BF16),
            pltpu.VMEM((size, width, width), BF16),
            gather_sems(size, parts),
            gather_sems(size, parts),
            dma((4,)),
            dma((4,)),
        ],
        compiler_params=params(2),
        name="convolve_project",
    )(attended, xg, affg, wo_all, w_glu_value, w_glu_gate, wp_all, depth_kernel, norms)


def solution(mesh):
    return jax.shard_map(
        on_device,
        mesh=mesh,
        in_specs=(
            P(("parts", "ctx"), "grid"),
            P("grid"),
            P("grid"),
            P(None, "grid"),
            P(None, "grid"),
            P(None, "grid"),
            P("grid", None),
            P("grid"),
            P("grid"),
            P(None, "grid"),
            P(None, "grid"),
            P(None, "grid"),
            P("grid"),
            P("grid"),
            P("grid", None),
        ),
        out_specs=P(("parts", "ctx"), "grid"),
        check_vma=False,
    )
```

time: 291 us -> 121 us (0.42)
  waiting for transfers between devices: 169 us -> 0 us
  Pallas kernels: 0 us -> 111 us
  matrix products: 52.1 us -> 0 us
  other arithmetic: 24 us -> 1.2 us
  between operations: 13.7 us -> 0.09 us
  blocking collectives: 12.1 us -> 0 us
  starting transfers between devices: 5.67 us -> 0 us
  local copies, waits for them, and re-layouts: 12.8 us -> 9 us
    all_gather x4 -> x0, waiting for transfers between devices: 112 us -> none  [the longest x2 43 us: project_normed(): block_piece = lax.all_gather(normed, 'grid', axis=1, tiled=True)]
    pallas_call x0 -> x3, Pallas kernels: none -> 111 us  [the longest x1 60.4 us: on_device(): pl.pallas_call(lambda *refs: attend_kernel(size, count, kv_parts, *refs),...]
    unnamed x8 -> x0, waiting for transfers between devices: 56.7 us -> none
    dot_general x15 -> x0, matrix products: 52.1 us -> none  [the longest x4 15.9 us: attend_block(): jnp.einsum('hqk,khd->qhd', soft_weights.astype(jnp.bfloat16), value_heads...]
    reduce_sum x6 -> x0, other arithmetic: 16.8 us -> none  [the longest x4 15.3 us: attend_block(): new_sum = row_sum * factor + jnp.sum(soft_weights, axis=2)]
    psum x2 -> x0, blocking collectives: 12.1 us -> none  [project_normed(): lax.psum((jnp.sum(values, axis=1), jnp.sum(values * values, axis=1)), 'gr...]
    dynamic_slice x12 -> x0, local copies, waits for them, and re-layouts: 6.31 us -> none  [the longest x8 5.55 us: loop_step(): lax.dynamic_slice_in_dim(value_rows, block_index * block_rows, block_rows...]
    convert_element_type x8 -> x0, other arithmetic: 6.03 us -> none  [the longest x2 2.93 us: project_normed(): (scaled * gain_shard.astype(jnp.float32) + shift_shard.astype(jnp.float32...]
  transfers between devices with their start and end apart: 8 -> 0, of which waited for: 7 -> 0; matrix products, arithmetic and copies ran while one was open for 2% -> 0% of each run, Pallas kernels for 0% -> 0%
where the time goes in v1:
time: 121 us
  Pallas kernels  111 us (92%)
  local copies, waits for them, and re-layouts  9 us (7%)
    pallas_call x1, Pallas kernels, on_device(): pl.pallas_call(lambda *refs: attend_kernel(size, count, kv_parts, *refs),...  60.4 us
    pallas_call x1, Pallas kernels, on_device(): pl.pallas_call(lambda *refs: last_kernel(size, count, parts, *refs), out_...  31.8 us
    pallas_call x1, Pallas kernels, on_device(): pl.pallas_call(lambda *refs: first_kernel(size, parts, *refs), out_shape=...  18.4 us
    unnamed x11, local copies, waits for them, and re-layouts  3.26 us
    another operation x4, local copies, waits for them, and re-layouts, on_device(): jnp.stack([norm1_gain, norm1_bias, norm2_gain, norm2_bias]).astype(F32)  2.73 us

profile of v1, /device:TPU:1, one launch (start us, length us, event | category | flops | bytes accessed | tf_op | source)
XLA Modules:
  0.0 120.8 jit_solution(877177599938387470)
XLA Ops:
  0.0 0.7 stack.24
  0.7 0.7 stack.25
  1.4 0.7 stack.26
  2.0 0.7 stack.27
  2.7 0.6 fusion.7.refs_1_
  3.3 0.0 copy-start
  3.3 18.4 %gather_project.1 = (bf16[4,512,384]{2,1,0:T(8,128)(2,1)}, f32[4,8,384]{2,1,0:T(8,128)}, bf16[512,384]{1,0:T(8,128)(2,1)}, bf16[2,512,384]{2,1,0:T(8,128)(2,1)}) custom-call(bf16[512,384]{1,0:T(8,128)(2,1)} %refs_0_.1, f32[8,384]{1,0:T(8,128)} %fusion.7.refs_1_, bf16[1536,384]{1,0:T(8,128)(2,1)} %refs_2_.1, bf16[1536,384]{1,0:T(8,128)(2,1)} %refs_3_.1, ...), custom_call_target="tpu_custom_call" | custom-call | tf_op jit(solution)/shard_map/gather_project/pallas_call | solution.py:567
  21.7 0.0 copy-done
  21.7 0.7 copy.16
  22.5 0.0 copy-start.1
  22.5 1.5 %copy.17 = bf16[384,4,384]{2,0,1:T(8,128)(2,1)} copy(bf16[384,4,384]{0,2,1:T(8,128)(2,1)S(1)} %bitcast.6) | data formatting | bytes 2359296 | tf_op jit(solution)/shard_map/reshape | solution.py:564
  24.0 0.0 copy-done.1
  24.0 0.7 copy.18
  24.7 1.5 %copy.19 = bf16[384,4,384]{2,0,1:T(8,128)(2,1)} copy(bf16[384,4,384]{0,2,1:T(8,128)(2,1)S(1)} %bitcast.7) | data formatting | bytes 2359296 | tf_op jit(solution)/shard_map/reshape | solution.py:565
  26.2 0.0 copy-start.2
  26.2 0.0 copy-start.3
  26.2 60.4 %attend_ring.1 = (bf16[512,384]{1,0:T(8,128)(2,1)}, bf16[4,4,384,384]{3,2,1,0:T(8,128)(2,1)}, bf16[4,384,384]{2,1,0:T(8,128)(2,1)}) custom-call(bf16[512,384]{1,0:T(8,128)(2,1)} %get-tuple-element.12.refs_0_, bf16[2,512,384]{2,1,0:T(8,128)(2,1)} %get-tuple-element.13.refs_1_, bf16[4,384,384]{2,1,0:T(8,128)(2,1)} %bitcast.4, bf16[4,384,384]{2,1,0:T(8,128)(2,1)} %bitcast.5), custom_call_target="tpu_custom_call" | custom-call | tf_op jit(solution)/shard_map/attend_ring/pallas_call | solution.py:584
  86.7 0.0 copy-done.2
  86.7 0.0 copy-done.3
  86.7 0.6 pad_maximum_fusion.refs_8_
  87.3 31.8 %convolve_project.1 = bf16[512,384]{1,0:T(8,128)(2,1)} custom-call(bf16[512,384]{1,0:T(8,128)(2,1)} %get-tuple-element.14.refs_0_, bf16[4,512,384]{2,1,0:T(8,128)(2,1)} %get-tuple-element.15.refs_1_, f32[4,8,384]{2,1,0:T(8,128)} %get-tuple-element.16.refs_2_, bf16[4,4,384,384]{3,2,1,0:T(8,128)(2,1)} %get-tuple-element.17.refs_3_, bf16[1536,384]{1,0:T(8,128)(2,1)} %refs_4_.3, ...), custom_call_target="tpu_custom_call" | custom-call | tf_op jit(solution)/shard_map/convolve_project/pallas_call | solution.py:609
  119.0 1.8 %copy.21 = bf16[512,384]{1,0:T(8,128)(2,1)} copy(bf16[512,384]{1,0:T(8,128)(2,1)} %convolve_project.1) | data formatting | bytes 786432
  (2 shorter events, 0.0 us)
Async XLA Ops:
  3.3 18.4 %copy-start = (bf16[384,1536]{1,0:T(8,128)(2,1)S(1)}, bf16[384,1536]{1,0:T(8,128)(2,1)}, u32[]{:S(2)}) copy-start(bf16[384,1536]{1,0:T(8,128)(2,1)} %param.21) | copy-start | bytes 3538948
  22.5 1.5 %copy-start.1 = (bf16[384,1536]{1,0:T(8,128)(2,1)S(1)}, bf16[384,1536]{1,0:T(8,128)(2,1)}, u32[]{:S(2)}) copy-start(bf16[384,1536]{1,0:T(8,128)(2,1)} %param.29) | copy-start | bytes 3538948
  26.2 60.4 %copy-start.2 = (f32[384]{0:T(512)S(1)}, f32[384]{0:T(512)}, u32[]{:S(2)}) copy-start(f32[384]{0:T(512)} %param.27) | copy-start | bytes 4612
  26.2 60.5 %copy-start.3 = (f32[384]{0:T(512)S(1)}, f32[384]{0:T(512)}, u32[]{:S(2)}) copy-start(f32[384]{0:T(512)} %param.28) | copy-start | bytes 4612

commit v2 on v1

v2 whole, which is shorter than its diff:
```python
import math

import jax
import jax.numpy as jnp
from jax import lax
from jax.experimental import pallas as pl
from jax.experimental.pallas import tpu as pltpu
from jax.sharding import PartitionSpec as P

HEAD_DIM = 64
KERNEL = 31
HALF = 15
EPSILON = 1e-05
LANES = 128
PAD = 16
MESH = pl.DeviceIdType.MESH
F32 = jnp.float32
BF16 = jnp.bfloat16
VMEM_LIMIT = 56 * 1024 * 1024


def remote(src, dst, send, recv, axis, index):
    return pltpu.make_async_remote_copy(
        src_ref=src,
        dst_ref=dst,
        send_sem=send,
        recv_sem=recv,
        device_id={axis: index},
        device_id_type=MESH,
    )


class GridGather:
    def __init__(self, size, sems):
        self.me = lax.axis_index("grid")
        self.chips = size // 2
        self.chip = self.me // 2
        self.core = self.me % 2
        self.mate = self.chip * 2 + 1 - self.core
        self.sems = sems

    def peer(self, step):
        return lax.rem(self.chip + step, self.chips) * 2 + self.core

    def source(self, step):
        return lax.rem(self.chip + self.chips - step, self.chips) * 2 + self.core

    def source_mate(self, step):
        return lax.rem(self.chip + self.chips - step, self.chips) * 2 + 1 - self.core

    def greet(self, barrier):
        pl.semaphore_signal(barrier, inc=1, device_id={"grid": self.mate}, device_id_type=MESH)
        for step in range(1, self.chips):
            pl.semaphore_signal(
                barrier, inc=1, device_id={"grid": self.peer(step)}, device_id_type=MESH
            )
        return self.chips

    def own(self, view, part, step):
        ref = view(self.me)
        target = self.mate if step == 0 else self.peer(step)
        return remote(ref, ref, self.sems.at[0, step, part], self.sems.at[1, step, part], "grid", target)

    def arrived(self, view, part, step):
        slot = self.mate if step == 0 else self.source(step)
        ref = view(slot)
        return remote(ref, ref, self.sems.at[0, step, part], self.sems.at[1, step, part], "grid", self.mate)

    def relay(self, view, part, step):
        ref = view(self.source(step))
        return remote(ref, ref, self.sems.at[2, step, part], self.sems.at[3, step, part], "grid", self.mate)

    def relayed(self, view, part, step):
        ref = view(self.source_mate(step))
        return remote(ref, ref, self.sems.at[2, step, part], self.sems.at[3, step, part], "grid", self.mate)

    def start(self, view, part):
        for step in range(1, self.chips):
            self.own(view, part, step).start()
        self.own(view, part, 0).start()

    def forward(self, view, part):
        for step in range(1, self.chips):
            self.arrived(view, part, step).wait_recv()
            self.relay(view, part, step).start()

    def finish(self, view, part):
        self.arrived(view, part, 0).wait_recv()
        for step in range(1, self.chips):
            self.relayed(view, part, step).wait_recv()

    def drain(self, view, part):
        for step in range(self.chips):
            self.own(view, part, step).wait_send()
        for step in range(1, self.chips):
            self.relay(view, part, step).wait_send()


def gather_sems(size, parts):
    return pltpu.SemaphoreType.DMA((4, size // 2, parts))


def normalize(pieces, gains, shifts):
    width = pieces[0].shape[1] * len(pieces)
    total = sum(jnp.sum(piece, axis=1, keepdims=True) for piece in pieces)
    mean = total / width
    centred = [piece - mean for piece in pieces]
    square = sum(jnp.sum(piece * piece, axis=1, keepdims=True) for piece in centred)
    scale = lax.rsqrt(square / width + EPSILON)
    return [
        (piece * scale * gain + shift).astype(BF16)
        for piece, gain, shift in zip(centred, gains, shifts)
    ]


def project(pieces, weight_ref):
    width = pieces[0].shape[1]
    if width % LANES == 0:
        return jnp.dot(
            jnp.concatenate(pieces, axis=1), weight_ref[...], preferred_element_type=F32
        )
    total = None
    for index, piece in enumerate(pieces):
        term = jnp.dot(
            piece, weight_ref[index * width : (index + 1) * width, :], preferred_element_type=F32
        )
        total = term if total is None else total + term
    return total


def attend_kernel(
    size, count, parts, x_ref, *refs,
):
    vector_refs, refs = refs[:6], refs[6:]
    (
        wq_hbm, wk_hbm, wv_hbm, wo_ref,
        att_ref, xown_ref, affg_ref, wog_ref,
        xg_ref, wq_ref, wk_ref, wv_ref, q_ref, keys_ref, values_ref, qm_ref, max_ref, acc_ref,
        x_sems, aff_sems, right_sems, left_sems, wo_sems, load_sems,
    ) = refs
    rows, width = x_ref.shape
    heads = width // HEAD_DIM
    step_rows = rows // parts
    ctx = lax.axis_index("ctx")
    gather = GridGather(size, x_sems)
    small = GridGather(size, aff_sems)
    weights = GridGather(size, wo_sems)
    me = gather.me
    has_left = ctx > 0
    has_right = ctx < count - 1
    loads = [
        pltpu.make_async_copy(src, dst, load_sems.at[index])
        for index, (src, dst) in enumerate(
            ((wq_hbm, wq_ref), (wk_hbm, wk_ref), (wv_hbm, wv_ref), (wo_ref, wog_ref.at[me]))
        )
    ]
    for load in loads:
        load.start()
    barrier = pltpu.get_barrier_semaphore()
    greeted = gather.greet(barrier)

    @pl.when(has_left)
    def _():
        pl.semaphore_signal(barrier, inc=1, device_id={"ctx": ctx - 1}, device_id_type=MESH)

    @pl.when(has_right)
    def _():
        pl.semaphore_signal(barrier, inc=1, device_id={"ctx": ctx + 1}, device_id_type=MESH)

    xg_ref[ctx, me] = x_ref[...]
    for index, vector_ref in enumerate(vector_refs):
        affg_ref[me, index : index + 1, :] = vector_ref[...].astype(F32).reshape(1, width)
    affg_ref[me, 6:8, :] = jnp.zeros((2, width), F32)
    inner = (ctx + count - 1) // count + (2 * count - 2 - ctx) // count
    pl.semaphore_wait(barrier, greeted + inner)

    def block(slot, part):
        return lambda index: xg_ref.at[slot, index, pl.ds(part * step_rows, step_rows), :]

    def line(sems, slot, part, target):
        ref = block(slot, part)(me)
        return remote(ref, ref, sems.at[0, slot, part], sems.at[1, slot, part], "ctx", target)

    def place(order):
        short = jnp.minimum(ctx, count - 1 - ctx)
        near = (order + 1) // 2
        both = jnp.where(order % 2 == 1, ctx - near, ctx + near)
        rest = jnp.where(2 * ctx > count - 1, ctx - (order - short), ctx + (order - short))
        return jnp.where(order <= 2 * short, both, rest)

    def small_view(slot):
        return affg_ref.at[slot]

    def wo_view(slot):
        return wog_ref.at[slot]

    def advance(order):
        slot = place(order)
        for part in range(parts):

            @pl.when(slot < ctx)
            def _():
                line(right_sems, slot, part, ctx - 1).wait_recv()

                @pl.when(has_right)
                def _():
                    line(right_sems, slot, part, ctx + 1).start()

            @pl.when(slot > ctx)
            def _():
                line(left_sems, slot, part, ctx + 1).wait_recv()

                @pl.when(has_left)
                def _():
                    line(left_sems, slot, part, ctx - 1).start()

            gather.start(block(slot, part), slot * parts + part)

    def relay(order):
        slot = place(order)
        for part in range(parts):
            gather.forward(block(slot, part), slot * parts + part)

    small.start(small_view, 0)
    for part in range(parts):
        gather.start(block(ctx, part), ctx * parts + part)

        @pl.when(has_right)
        def _():
            line(right_sems, ctx, part, ctx + 1).start()

        @pl.when(has_left)
        def _():
            line(left_sems, ctx, part, ctx - 1).start()

    small.forward(small_view, 0)
    small.finish(small_view, 0)
    for load in loads:
        load.wait()
    scale = math.log2(math.e) / math.sqrt(HEAD_DIM)

    def prepare(slot, part):
        gather.finish(block(slot, part), slot * parts + part)
        span = slice(part * step_rows, (part + 1) * step_rows)
        gains = [affg_ref[index, 0:1, :] for index in range(size)]
        shifts = [affg_ref[index, 1:2, :] for index in range(size)]
        pieces = [xg_ref[slot, index, span, :].astype(F32) for index in range(size)]
        normed = normalize(pieces, gains, shifts)
        keys_ref[span, :] = project(normed, wk_ref).astype(BF16)
        values_ref[span, :] = project(normed, wv_ref).astype(BF16)
        return span, normed

    spans = []
    for head in range(heads):
        low = head * HEAD_DIM // LANES * LANES
        spans.append((low, min(low + LANES, width)))

    def attend(first):
        for head in range(heads):
            low, high = spans[head]
            keys = keys_ref[:, low:high]
            values = values_ref[:, low:high]
            extra = [jnp.ones((rows, LANES), BF16)]
            if high - low < LANES:
                extra = [jnp.zeros((rows, LANES - (high - low)), BF16)] + extra
            values = jnp.concatenate([values] + extra, axis=1)
            scores = lax.dot_general(
                qm_ref[head, :, 0 : high - low], keys, (((1,), (1,)), ((), ())),
                preferred_element_type=F32,
            )
            peak = jnp.max(scores, axis=1, keepdims=True)
            if first:
                peak = jnp.broadcast_to(peak, (rows, LANES))
            else:
                old = max_ref[head]
                peak = jnp.maximum(old, peak)
            soft = jnp.exp2(scores - jnp.concatenate([peak] * (rows // LANES), axis=1)).astype(BF16)
            mixed = jnp.dot(soft, values, preferred_element_type=F32)
            if first:
                acc_ref[head] = mixed
            else:
                factor = jnp.exp2(old - peak)
                acc_ref[head] = acc_ref[head] * jnp.concatenate([factor, factor], axis=1) + mixed
            max_ref[head] = peak

    relay(0)
    advance(1)
    for part in range(parts):
        span, normed = prepare(ctx, part)
        q_ref[span, :] = (project(normed, wq_ref) * scale).astype(BF16)
    keep = pltpu.make_async_copy(xg_ref.at[ctx], xown_ref, load_sems.at[4])
    keep.start()
    advance(2)
    relay(1)
    for head in range(heads):
        low, high = spans[head]
        pair = q_ref[:, low:high]
        lane = lax.broadcasted_iota(jnp.int32, pair.shape, 1)
        inside = lane // HEAD_DIM == (head * HEAD_DIM - low) // HEAD_DIM
        qm_ref[head, :, 0 : high - low] = jnp.where(inside, pair, jnp.zeros_like(pair))
    attend(True)

    @pl.loop(1, count)
    def _(order):
        slot = place(order)
        for part in range(parts):
            prepare(slot, part)

        @pl.when(order + 2 < count)
        def _():
            advance(order + 2)

        @pl.when(order == count - 3)
        def _():
            weights.start(wo_view, 0)

        @pl.when(order + 1 < count)
        def _():
            relay(order + 1)

        attend(False)

    for pair in range((heads + 1) // 2):
        low, high = spans[2 * pair]
        results = [
            acc_ref[head, :, 0:LANES] / acc_ref[head, :, LANES : 2 * LANES]
            for head in range(2 * pair, min(2 * pair + 2, heads))
        ]
        if len(results) == 2:
            lane = lax.broadcasted_iota(jnp.int32, (rows, LANES), 1)
            mixed = jnp.where(lane < HEAD_DIM, results[0], results[1])
        else:
            mixed = results[0]
        att_ref[:, low:high] = mixed[:, 0 : high - low].astype(BF16)

    weights.forward(wo_view, 0)
    weights.finish(wo_view, 0)
    weights.drain(wo_view, 0)
    small.drain(small_view, 0)
    keep.wait()

    @pl.loop(0, count)
    def _(slot):
        for part in range(parts):
            gather.drain(block(slot, part), slot * parts + part)

            @pl.when(has_right & (slot <= ctx))
            def _():
                line(right_sems, slot, part, ctx + 1).wait_send()

            @pl.when(has_left & (slot >= ctx))
            def _():
                line(left_sems, slot, part, ctx - 1).wait_send()


def last_kernel(
    size, count, parts, att_ref, xg_ref, affg_ref, wog_hbm, wgv_hbm, wgg_hbm, wp_hbm,
    taps_ref, out_ref,
    attg_ref, actg_ref, mid_ref, gated_ref, wo_ref, wgv_ref, wgg_ref, wp_ref,
    att_sems, act_sems, halo_sems, load_sems, wp_sems,
):
    rows, width = att_ref.shape
    step_rows = rows // parts
    ctx = lax.axis_index("ctx")
    attended = GridGather(size, att_sems)
    activated = GridGather(size, act_sems)
    me = attended.me
    has_left = ctx > 0
    has_right = ctx < count - 1

    def wp_block(index):
        if len(wp_hbm.shape) == 3:
            return wp_hbm.at[index]
        return wp_hbm.at[:, pl.ds(pl.multiple_of(index * width, LANES), width)]

    def wp_slot(index):
        return wp_ref.at[pl.ds(pl.multiple_of(index * width, HEAD_DIM), width), :]

    def send_wp(step):
        target = lax.rem(me + step, size)
        return remote(
            wp_block(target), wp_slot(me), wp_sems.at[0, step], wp_sems.at[1, step], "grid", target
        )

    def take_wp(step):
        source = lax.rem(me + size - step, size)
        return remote(
            wp_block(me), wp_slot(source), wp_sems.at[0, step], wp_sems.at[1, step], "grid", source
        )

    loads = [
        pltpu.make_async_copy(src, dst, load_sems.at[index])
        for index, (src, dst) in enumerate(
            ((wog_hbm, wo_ref), (wgv_hbm, wgv_ref), (wgg_hbm, wgg_ref), (wp_block(me), wp_slot(me)))
        )
    ]
    for load in loads:
        load.start()
    barrier = pltpu.get_barrier_semaphore()
    greeted = size - 1
    for step in range(1, size):
        pl.semaphore_signal(
            barrier, inc=1, device_id={"grid": lax.rem(me + step, size)}, device_id_type=MESH
        )

    @pl.when(has_left)
    def _():
        pl.semaphore_signal(barrier, inc=1, device_id={"ctx": ctx - 1}, device_id_type=MESH)

    @pl.when(has_right)
    def _():
        pl.semaphore_signal(barrier, inc=1, device_id={"ctx": ctx + 1}, device_id_type=MESH)

    attg_ref[me] = att_ref[...]
    inner = (ctx + count - 1) // count + (2 * count - 2 - ctx) // count
    pl.semaphore_wait(barrier, greeted + inner)

    def view(buffer, part):
        return lambda slot: buffer.at[slot, pl.ds(part * step_rows, step_rows), :]

    for part in range(parts):
        attended.start(view(attg_ref, part), part)
    for step in range(1, size):
        send_wp(step).start()

    @pl.when(jnp.logical_not(has_left))
    def _():
        gated_ref[0:PAD, :] = jnp.zeros((PAD, width), F32)

    @pl.when(jnp.logical_not(has_right))
    def _():
        gated_ref[PAD + rows : 2 * PAD + rows, :] = jnp.zeros((PAD, width), F32)

    def halo_left(index):
        return remote(
            gated_ref.at[PAD : 2 * PAD, :], gated_ref.at[PAD + rows : 2 * PAD + rows, :],
            halo_sems.at[0], halo_sems.at[1], "ctx", index,
        )

    def halo_right(index):
        return remote(
            gated_ref.at[rows : rows + PAD, :], gated_ref.at[0:PAD, :],
            halo_sems.at[2], halo_sems.at[3], "ctx", index,
        )

    attended.forward(view(attg_ref, 0), 0)
    for load in loads:
        load.wait()
    gains = [affg_ref[index, 2:3, :] for index in range(size)]
    shifts = [affg_ref[index, 3:4, :] for index in range(size)]
    for part in range(parts):
        if part + 1 < parts:
            attended.forward(view(attg_ref, part + 1), part + 1)
        attended.finish(view(attg_ref, part), part)
        span = slice(part * step_rows, (part + 1) * step_rows)
        products = project([attg_ref[index, span, :] for index in range(size)], wo_ref)
        pieces = []
        for column in range(size):
            total = products[:, column * width : (column + 1) * width]
            middle = (xg_ref[column, span, :].astype(F32) + total).astype(BF16)
            mid_ref[column, span, :] = middle
            pieces.append(middle.astype(F32))
        normed = normalize(pieces, gains, shifts)
        gate = project(normed, wgg_ref)
        value = project(normed, wgv_ref)
        gated = (value * (1.0 / (1.0 + jnp.exp(-gate)))).astype(BF16)
        gated_ref[PAD + part * step_rows : PAD + (part + 1) * step_rows, :] = gated.astype(F32)
        if part == 0:

            @pl.when(has_left)
            def _():
                halo_left(ctx - 1).start()

    @pl.when(has_right)
    def _():
        halo_right(ctx + 1).start()

    block_rows = min(32, step_rows)
    inner_parts = list(range(1, parts - 1))
    for order, part in enumerate(inner_parts + [0] + ([parts - 1] if parts > 1 else [])):
        if order == len(inner_parts):

            @pl.when(has_left)
            def _():
                halo_right(ctx - 1).wait_recv()

            @pl.when(has_right)
            def _():
                halo_left(ctx + 1).wait_recv()

        @pl.loop(0, step_rows // block_rows)
        def _(block):
            base = pl.multiple_of(part * step_rows + block * block_rows, block_rows)
            window = gated_ref[pl.ds(base, block_rows + 2 * PAD), :]
            total = jnp.zeros((block_rows, width), F32)
            for tap in range(KERNEL):
                low = tap + PAD - HALF
                total = total + taps_ref[tap : tap + 1, :] * window[low : low + block_rows, :]
            scaled = total * affg_ref[me, 4:5, :] + affg_ref[me, 5:6, :]
            result = scaled / (1.0 + jnp.exp(-scaled))
            actg_ref[me, pl.ds(base, block_rows), :] = result.astype(BF16)

        activated.start(view(actg_ref, part), part)

    sequence = inner_parts + [0] + ([parts - 1] if parts > 1 else [])
    activated.forward(view(actg_ref, sequence[0]), sequence[0])
    for step in range(1, size):
        take_wp(step).wait_recv()
    for order, part in enumerate(sequence):
        if order + 1 < parts:
            activated.forward(view(actg_ref, sequence[order + 1]), sequence[order + 1])
        activated.finish(view(actg_ref, part), part)
        span = slice(part * step_rows, (part + 1) * step_rows)
        total = mid_ref[me, span, :].astype(F32)
        total = total + project([actg_ref[index, span, :] for index in range(size)], wp_ref)
        out_ref[span, :] = total.astype(BF16)

    for part in range(parts):
        attended.drain(view(attg_ref, part), part)
        activated.drain(view(actg_ref, part), part)
    for step in range(1, size):
        send_wp(step).wait_send()

    @pl.when(has_left)
    def _():
        halo_left(ctx - 1).wait_send()

    @pl.when(has_right)
    def _():
        halo_right(ctx + 1).wait_send()


def params(number):
    return pltpu.CompilerParams(
        collective_id=number, has_side_effects=True, vmem_limit_bytes=VMEM_LIMIT
    )


def on_device(
    frames_in,
    norm1_gain,
    norm1_bias,
    w_query,
    w_key,
    w_value,
    w_out,
    norm2_gain,
    norm2_bias,
    w_glu_value,
    w_glu_gate,
    depth_kernel,
    bn_scale,
    bn_shift,
    w_proj,
):
    size = lax.axis_size("grid")
    count = lax.axis_size("ctx")
    rows, width = frames_in.shape
    full = width * size
    heads = width // HEAD_DIM
    vmem = pl.BlockSpec(memory_space=pltpu.VMEM)
    anywhere = pl.BlockSpec(memory_space=pl.ANY)
    dma = pltpu.SemaphoreType.DMA
    parts = 4

    def shape(dims, dtype=BF16):
        return jax.ShapeDtypeStruct(dims, dtype)

    wp_blocks = w_proj
    if width % LANES:
        wp_blocks = jnp.transpose(w_proj.reshape(width, size, width), (1, 0, 2))
    line_parts = 2
    weight = pltpu.VMEM((full, width), BF16)
    attended, frames_all, affine, wo_all = pl.pallas_call(
        lambda *refs: attend_kernel(size, count, line_parts, *refs),
        out_shape=(
            shape((rows, width)),
            shape((size, rows, width)),
            shape((size, 8, width), F32),
            shape((size, width, full)),
        ),
        in_specs=[vmem] * 7 + [anywhere] * 4,
        out_specs=(vmem, anywhere, vmem, anywhere),
        scratch_shapes=[
            pltpu.VMEM((count, size, rows, width), BF16),
            weight,
            weight,
            weight,
            pltpu.VMEM((rows, width), BF16),
            pltpu.VMEM((rows, width), BF16),
            pltpu.VMEM((rows, width), BF16),
            pltpu.VMEM((heads, rows, LANES), BF16),
            pltpu.VMEM((heads, rows, LANES), F32),
            pltpu.VMEM((heads, rows, 2 * LANES), F32),
            gather_sems(size, count * line_parts),
            gather_sems(size, 1),
            dma((2, count, line_parts)),
            dma((2, count, line_parts)),
            gather_sems(size, 1),
            dma((5,)),
        ],
        compiler_params=params(1),
        name="attend_ring",
    )(
        frames_in, norm1_gain, norm1_bias, norm2_gain, norm2_bias, bn_scale, bn_shift,
        w_query, w_key, w_value, w_out,
    )

    return pl.pallas_call(
        lambda *refs: last_kernel(size, count, parts, *refs),
        out_shape=shape((rows, width)),
        in_specs=[vmem, vmem, vmem] + [anywhere] * 4 + [vmem],
        out_specs=vmem,
        scratch_shapes=[
            pltpu.VMEM((size, rows, width), BF16),
            pltpu.VMEM((size, rows, width), BF16),
            pltpu.VMEM((size, rows, width), BF16),
            pltpu.VMEM((rows + 2 * PAD, width), F32),
            pltpu.VMEM((full, full), BF16),
            pltpu.VMEM((full, width), BF16),
            pltpu.VMEM((full, width), BF16),
            pltpu.VMEM((full, width), BF16),
            gather_sems(size, parts),
            gather_sems(size, parts),
            dma((4,)),
            dma((4,)),
            dma((2, size)),
        ],
        compiler_params=params(2),
        name="convolve_project",
    )(
        attended, frames_all, affine, wo_all.reshape(full, full), w_glu_value, w_glu_gate,
        wp_blocks, depth_kernel,
    )


def solution(mesh):
    return jax.shard_map(
        on_device,
        mesh=mesh,
        in_specs=(
            P(("parts", "ctx"), "grid"),
            P("grid"),
            P("grid"),
            P(None, "grid"),
            P(None, "grid"),
            P(None, "grid"),
            P("grid", None),
            P("grid"),
            P("grid"),
            P(None, "grid"),
            P(None, "grid"),
            P(None, "grid"),
            P("grid"),
            P("grid"),
            P("grid", None),
        ),
        out_specs=P(("parts", "ctx"), "grid"),
        check_vma=False,
    )
```

time: 121 us -> 139 us (1.15)
  Pallas kernels: 111 us -> 137 us
  local copies, waits for them, and re-layouts: 9 us -> 1.78 us
    pallas_call x2 -> x1, Pallas kernels: 78.8 us -> 101 us  [on_device(): pl.pallas_call(lambda *refs: attend_kernel(size, count, line_parts, *refs...]
    pallas_call x1, Pallas kernels: 31.8 us -> 36.9 us  [on_device(): pl.pallas_call(lambda *refs: last_kernel(size, count, parts, *refs), out_...]
    reshape x2 -> x0, local copies, waits for them, and re-layouts: 3 us -> none  [the longest x1 1.51 us: on_device(): wo_blocks = jnp.transpose(w_out.reshape(width, size, width), (1, 0, 2))]
    another operation x6 -> x0, local copies, waits for them, and re-layouts: 2.73 us -> none  [the longest x4 2.73 us: on_device(): jnp.stack([norm1_gain, norm1_bias, norm2_gain, norm2_bias]).astype(F32)]
    unnamed x11 -> x1, local copies, waits for them, and re-layouts: 3.26 us -> 1.78 us
where the time goes in v2:
time: 139 us
  Pallas kernels  137 us (99%)
  local copies, waits for them, and re-layouts  1.78 us (1%)
    pallas_call x1, Pallas kernels, on_device(): pl.pallas_call(lambda *refs: attend_kernel(size, count, line_parts, *refs...  101 us
    pallas_call x1, Pallas kernels, on_device(): pl.pallas_call(lambda *refs: last_kernel(size, count, parts, *refs), out_...  36.9 us

profile of v2, /device:TPU:1, one launch (start us, length us, event | category | flops | bytes accessed | tf_op | source)
XLA Modules:
  0.0 139.3 jit_solution(16333644409196808087)
XLA Ops:
  0.0 100.6 %attend_ring.1 = (bf16[512,384]{1,0:T(8,128)(2,1)}, bf16[4,512,384]{2,1,0:T(8,128)(2,1)}, f32[4,8,384]{2,1,0:T(8,128)}, bf16[4,384,1536]{2,1,0:T(8,128)(2,1)}) custom-call(bf16[512,384]{1,0:T(8,128)(2,1)} %refs_0_.1, bf16[384]{0:T(512)(128)(2,1)} %refs_1_.1, bf16[384]{0:T(512)(128)(2,1)} %refs_2_.1, bf16[384]{0:T(512)(128)(2,1)} %refs_3_.1, ...), custom_call_target="tpu_custom_call" | custom-call | tf_op jit(solution)/shard_map/attend_ring/pallas_call | solution.py:574
  100.6 36.9 %convolve_project.1 = bf16[512,384]{1,0:T(8,128)(2,1)} custom-call(bf16[512,384]{1,0:T(8,128)(2,1)} %get-tuple-element.9.refs_0_, bf16[4,512,384]{2,1,0:T(8,128)(2,1)} %get-tuple-element.10.refs_1_, f32[4,8,384]{2,1,0:T(8,128)} %get-tuple-element.11.refs_2_, bf16[1536,1536]{1,0:T(8,128)(2,1)} %bitcast.1, bf16[1536,384]{1,0:T(8,128)(2,1)} %refs_4_.3, ...), custom_call_target="tpu_custom_call" | custom-call | tf_op jit(solution)/shard_map/convolve_project/pallas_call | solution.py:609
  137.5 1.8 %copy.17 = bf16[512,384]{1,0:T(8,128)(2,1)} copy(bf16[512,384]{1,0:T(8,128)(2,1)} %convolve_project.1) | data formatting | bytes 786432

commit v3 on v1

--- a/solution.py
+++ b/solution.py
@@ -115,6 +115,10 @@
 
 def project(pieces, weight_ref):
     width = pieces[0].shape[1]
+    if width % LANES == 0:
+        return jnp.dot(
+            jnp.concatenate(pieces, axis=1), weight_ref[...], preferred_element_type=F32
+        )
     total = None
     for index, piece in enumerate(pieces):
         term = jnp.dot(
@@ -124,28 +128,73 @@
     return total
 
 
-def first_kernel(
-    size, parts, x_ref, affine_ref, wq_hbm, wk_hbm, wv_hbm,
-    xg_ref, affg_ref, q_ref, kv_ref,
-    wq_ref, wk_ref, wv_ref, sems, aff_sems, load_sems,
+def attend_kernel(
+    size, count, parts, x_ref, *refs,
 ):
-    rows = x_ref.shape[0]
+    vector_refs, refs = refs[:6], refs[6:]
+    (
+        wq_hbm, wk_hbm, wv_hbm, wo_ref, wp_ref,
+        att_ref, xg_ref, affg_ref, wog_ref, wpg_ref,
+        wq_ref, wk_ref, wv_ref, q_ref, kvg_ref, qm_ref, max_ref, acc_ref,
+        x_sems, aff_sems, right_sems, left_sems, wo_sems, wp_sems, load_sems, matrix_sems,
+    ) = refs
+    rows, width = x_ref.shape
+    heads = width // HEAD_DIM
     step_rows = rows // parts
-    gather = GridGather(size, sems)
+    ctx = lax.axis_index("ctx")
+    gather = GridGather(size, wo_sems)
+    frames = GridGather(size, x_sems)
     small = GridGather(size, aff_sems)
-    loads = [
-        pltpu.make_async_copy(src, dst, load_sems.at[index])
+    me = gather.me
+    has_left = ctx > 0
+    has_right = ctx < count - 1
+    matrices = [
+        pltpu.make_async_copy(src, dst, matrix_sems.at[index])
         for index, (src, dst) in enumerate(((wq_hbm, wq_ref), (wk_hbm, wk_ref), (wv_hbm, wv_ref)))
     ]
-    for load in loads:
+    for load in matrices:
         load.start()
     barrier = pltpu.get_barrier_semaphore()
-    count = gather.greet(barrier)
-    xg_ref[gather.me] = x_ref[...]
-    affg_ref[gather.me] = affine_ref[...]
-    pl.semaphore_wait(barrier, count)
-
-    def view(part):
+    for step in range(1, size):
+        pl.semaphore_signal(
+            barrier, inc=1, device_id={"grid": lax.rem(me + step, size)}, device_id_type=MESH
+        )
+
+    @pl.when(has_left)
+    def _():
+        pl.semaphore_signal(barrier, inc=1, device_id={"ctx": ctx - 1}, device_id_type=MESH)
+
+    @pl.when(has_right)
+    def _():
+        pl.semaphore_signal(barrier, inc=1, device_id={"ctx": ctx + 1}, device_id_type=MESH)
+
+    xg_ref[me] = x_ref[...]
+    for index, vector_ref in enumerate(vector_refs):
+        affg_ref[me, index : index + 1, :] = vector_ref[...].astype(F32).reshape(1, width)
+    affg_ref[me, 6:8, :] = jnp.zeros((2, width), F32)
+    inner = (ctx + count - 1) // count + (2 * count - 2 - ctx) // count
+    pl.semaphore_wait(barrier, size - 1 + inner)
+
+    def block(slot, part):
+        return kvg_ref.at[slot, :, pl.ds(part * step_rows, step_rows), :]
+
+    def to_right(step, part):
+        ref = block(ctx - step, part)
+        return remote(ref, ref, right_sems.at[0, step, part], right_sems.at[1, step, part], "ctx", ctx + 1)
+
+    def from_left(step, part):
+        ref = block(ctx - 1 - step, part)
+        return remote(ref, ref, right_sems.at[0, step, part], right_sems.at[1, step, part], "ctx", ctx - 1)
+
+    def to_left(step, part):
+        ref = block(ctx + step, part)
+        return remote(ref, ref, left_sems.at[0, step, part], left_sems.at[1, step, part], "ctx", ctx - 1)
+
+    def from_right(step, part):
+        ref = block(ctx + 1 + step, part)
+        return remote(ref, ref, left_sems.at[0, step, part], left_sems.at[1, step, part], "ctx", ctx + 1)
+
+    def frames_view(part):
         return lambda slot: xg_ref.at[slot, pl.ds(part * step_rows, step_rows), :]
 
     def small_view(slot):
@@ -153,81 +202,25 @@
 
     small.start(small_view, 0)
     for part in range(parts):
-        gather.start(view(part), part)
+        frames.start(frames_view(part), part)
     small.forward(small_view, 0)
-    gather.forward(view(0), 0)
+    frames.forward(frames_view(0), 0)
     small.finish(small_view, 0)
-    for load in loads:
+    for load in matrices:
         load.wait()
     gains = [affg_ref[index, 0:1, :] for index in range(size)]
     shifts = [affg_ref[index, 1:2, :] for index in range(size)]
     scale = math.log2(math.e) / math.sqrt(HEAD_DIM)
     for part in range(parts):
         if part + 1 < parts:
-            gather.forward(view(part + 1), part + 1)
-        gather.finish(view(part), part)
+            frames.forward(frames_view(part + 1), part + 1)
+        frames.finish(frames_view(part), part)
         span = slice(part * step_rows, (part + 1) * step_rows)
-        pieces = [xg_ref[index, span, :].astype(F32) for index in range(size)]
-        normed = normalize(pieces, gains, shifts)
-        q_ref[span, :] = (project(normed, wq_ref) * scale).astype(BF16)
-        kv_ref[0, span, :] = project(normed, wk_ref).astype(BF16)
-        kv_ref[1, span, :] = project(normed, wv_ref).astype(BF16)
-    small.drain(small_view, 0)
-    for part in range(parts):
-        gather.drain(view(part), part)
-
-
-def attend_kernel(
-    size, count, parts, q_ref, kv_ref, wo_ref, wp_ref,
-    att_ref, wog_ref, wpg_ref,
-    kvg_ref, qm_ref, max_ref, acc_ref, right_sems, left_sems, wo_sems, wp_sems, load_sems,
-):
-    rows, width = q_ref.shape
-    heads = width // HEAD_DIM
-    step_rows = rows // parts
-    ctx = lax.axis_index("ctx")
-    gather = GridGather(size, wo_sems)
-    me = gather.me
-    has_left = ctx > 0
-    has_right = ctx < count - 1
-    barrier = pltpu.get_barrier_semaphore()
-    for step in range(1, size):
-        pl.semaphore_signal(
-            barrier, inc=1, device_id={"grid": lax.rem(me + step, size)}, device_id_type=MESH
+        normed = normalize(
+            [xg_ref[index, span, :].astype(F32) for index in range(size)], gains, shifts
         )
-
-    @pl.when(has_left)
-    def _():
-        pl.semaphore_signal(barrier, inc=1, device_id={"ctx": ctx - 1}, device_id_type=MESH)
-
-    @pl.when(has_right)
-    def _():
-        pl.semaphore_signal(barrier, inc=1, device_id={"ctx": ctx + 1}, device_id_type=MESH)
-
-    kvg_ref[ctx] = kv_ref[...]
-    inner = (ctx + count - 1) // count + (2 * count - 2 - ctx) // count
-    pl.semaphore_wait(barrier, size - 1 + inner)
-
-    def block(slot, part):
-        return kvg_ref.at[slot, :, pl.ds(part * step_rows, step_rows), :]
-
-    def to_right(step, part):
-        ref = block(ctx - step, part)
-        return remote(ref, ref, right_sems.at[0, step, part], right_sems.at[1, step, part], "ctx", ctx + 1)
-
-    def from_left(step, part):
-        ref = block(ctx - 1 - step, part)
-        return remote(ref, ref, right_sems.at[0, step, part], right_sems.at[1, step, part], "ctx", ctx - 1)
-
-    def to_left(step, part):
-        ref = block(ctx + step, part)
-        return remote(ref, ref, left_sems.at[0, step, part], left_sems.at[1, step, part], "ctx", ctx - 1)
-
-    def from_right(step, part):
-        ref = block(ctx + 1 + step, part)
-        return remote(ref, ref, left_sems.at[0, step, part], left_sems.at[1, step, part], "ctx", ctx + 1)
-
-    for part in range(parts):
+        kvg_ref[ctx, 0, span, :] = project(normed, wk_ref).astype(BF16)
+        kvg_ref[ctx, 1, span, :] = project(normed, wv_ref).astype(BF16)
 
         @pl.when(has_right)
         def _():
@@ -237,6 +230,8 @@
         def _():
             to_left(0, part).start()
 
+        q_ref[span, :] = (project(normed, wq_ref) * scale).astype(BF16)
+
     def wo_view(slot):
         return wog_ref.at[slot]
 
@@ -244,15 +239,20 @@
         target = gather.mate if step == 0 else gather.peer(step)
         remote(wo_ref, wog_ref.at[me], wo_sems.at[0, step, 0], wo_sems.at[1, step, 0], "grid", target).start()
 
+    def wp_block(index):
+        if len(wp_ref.shape) == 3:
+            return wp_ref.at[index]
+        return wp_ref.at[:, pl.ds(pl.multiple_of(index * width, LANES), width)]
+
     def send_wp(step):
         target = lax.rem(me + step, size)
-        return remote(wp_ref.at[target], wpg_ref.at[me], wp_sems.at[0, step], wp_sems.at[1, step], "grid", target)
+        return remote(wp_block(target), wpg_ref.at[me], wp_sems.at[0, step], wp_sems.at[1, step], "grid", target)
 
     for step in range(1, size):
         send_wp(step).start()
     loads = [
         pltpu.make_async_copy(wo_ref, wog_ref.at[me], load_sems.at[0]),
-        pltpu.make_async_copy(wp_ref.at[me], wpg_ref.at[me], load_sems.at[1]),
+        pltpu.make_async_copy(wp_block(me), wpg_ref.at[me], load_sems.at[1]),
     ]
     for load in loads:
         load.start()
@@ -344,6 +344,9 @@
             mixed = results[0]
         att_ref[:, low:high] = mixed[:, 0 : high - low].astype(BF16)
 
+    small.drain(small_view, 0)
+    for part in range(parts):
+        frames.drain(frames_view(part), part)
     gather.finish(wo_view, 0)
     for step in range(gather.chips):
         target = gather.mate if step == 0 else gather.peer(step)
@@ -353,7 +356,7 @@
     for step in range(1, size):
         send_wp(step).wait_send()
         source = lax.rem(me + size - step, size)
-        remote(wp_ref.at[me], wpg_ref.at[source], wp_sems.at[0, step], wp_sems.at[1, step], "grid", source).wait_recv()
+        remote(wp_block(me), wpg_ref.at[source], wp_sems.at[0, step], wp_sems.at[1, step], "grid", source).wait_recv()
     for load in loads:
         load.wait()
 
@@ -372,7 +375,7 @@
 
 def last_kernel(
     size, count, parts, att_ref, xg_ref, affg_ref, wog_hbm, wgv_hbm, wgg_hbm, wpg_hbm,
-    taps_ref, bn_ref, out_ref,
+    taps_ref, out_ref,
     attg_ref, actg_ref, mid_ref, gated_ref, wo_ref, wgv_ref, wgg_ref, wp_ref,
     att_sems, act_sems, halo_sems, load_sems,
 ):
@@ -444,14 +447,11 @@
         attended.finish(view(attg_ref, part), part)
         span = slice(part * step_rows, (part + 1) * step_rows)
         sources = [attg_ref[index, span, :] for index in range(size)]
+        products = project(sources, wo_ref)
         pieces = []
         for column in range(size):
-            total = xg_ref[column, span, :].astype(F32)
-            for index in range(size):
-                total = total + jnp.dot(
-                    sources[index], wo_ref[index, column], preferred_element_type=F32
-                )
-            middle = total.astype(BF16)
+            total = products[:, column * width : (column + 1) * width]
+            middle = (xg_ref[column, span, :].astype(F32) + total).astype(BF16)
             mid_ref[column, span, :] = middle
             pieces.append(middle.astype(F32))
         normed = normalize(pieces, gains, shifts)
@@ -490,7 +490,7 @@
             for tap in range(KERNEL):
                 low = tap + PAD - HALF
                 total = total + taps_ref[tap : tap + 1, :] * window[low : low + block_rows, :]
-            scaled = total * bn_ref[0:1, :] + bn_ref[1:2, :]
+            scaled = total * affg_ref[me, 4:5, :] + affg_ref[me, 5:6, :]
             result = scaled / (1.0 + jnp.exp(-scaled))
             actg_ref[me, pl.ds(base, block_rows), :] = result.astype(BF16)
 
@@ -504,10 +504,7 @@
         activated.finish(view(actg_ref, part), part)
         span = slice(part * step_rows, (part + 1) * step_rows)
         total = mid_ref[me, span, :].astype(F32)
-        for index in range(size):
-            total = total + jnp.dot(
-                actg_ref[index, span, :], wp_ref[index], preferred_element_type=F32
-            )
+        total = total + project([actg_ref[index, span, :] for index in range(size)], wp_ref)
         out_ref[span, :] = total.astype(BF16)
 
     for part in range(parts):
@@ -559,67 +556,60 @@
     def shape(dims, dtype=BF16):
         return jax.ShapeDtypeStruct(dims, dtype)
 
-    affine = jnp.stack([norm1_gain, norm1_bias, norm2_gain, norm2_bias]).astype(F32)
-    affine = jnp.pad(affine, ((0, 4), (0, 0)))
-    wo_blocks = jnp.transpose(w_out.reshape(width, size, width), (1, 0, 2))
-    wp_blocks = jnp.transpose(w_proj.reshape(width, size, width), (1, 0, 2))
-
-    xg, affg, queries, key_values = pl.pallas_call(
-        lambda *refs: first_kernel(size, parts, *refs),
+    wp_blocks = w_proj
+    if width % LANES:
+        wp_blocks = jnp.transpose(w_proj.reshape(width, size, width), (1, 0, 2))
+    weight = pltpu.VMEM((full, width), BF16)
+    attended, xg, affg, wo_all, wp_all = pl.pallas_call(
+        lambda *refs: attend_kernel(size, count, parts, *refs),
         out_shape=(
+            shape((rows, width)),
             shape((size, rows, width)),
             shape((size, 8, width), F32),
-            shape((rows, width)),
-            shape((2, rows, width)),
-        ),
-        in_specs=[vmem, vmem, anywhere, anywhere, anywhere],
-        out_specs=(vmem,) * 4,
-        scratch_shapes=[pltpu.VMEM((full, width), BF16)] * 3
-        + [gather_sems(size, parts), gather_sems(size, 1), dma((3,))],
-        compiler_params=params(0),
-        name="gather_project",
-    )(frames_in, affine, w_query, w_key, w_value)
-
-    kv_parts = 2
-    attended, wo_all, wp_all = pl.pallas_call(
-        lambda *refs: attend_kernel(size, count, kv_parts, *refs),
-        out_shape=(
-            shape((rows, width)),
-            shape((size, size, width, width)),
+            shape((size, width, full)),
             shape((size, width, width)),
         ),
-        in_specs=[vmem, vmem, anywhere, anywhere],
-        out_specs=(vmem, anywhere, anywhere),
+        in_specs=[vmem] * 7 + [anywhere] * 5,
+        out_specs=(vmem, vmem, vmem, anywhere, anywhere),
         scratch_shapes=[
+            weight,
+            weight,
+            weight,
+            pltpu.VMEM((rows, width), BF16),
             pltpu.VMEM((count, 2, rows, width), BF16),
             pltpu.VMEM((heads, rows, LANES), BF16),
             pltpu.VMEM((heads, rows, LANES), F32),
             pltpu.VMEM((heads, rows, 2 * LANES), F32),
-            dma((2, count, kv_parts)),
-            dma((2, count, kv_parts)),
+            gather_sems(size, parts),
+            gather_sems(size, 1),
+            dma((2, count, parts)),
+            dma((2, count, parts)),
             gather_sems(size, 1),
             dma((2, size)),
             dma((2,)),
+            dma((3,)),
         ],
         compiler_params=params(1),
         name="attend_ring",
-    )(queries, key_values, wo_blocks, wp_blocks)
-
-    norms = jnp.stack([bn_scale, bn_shift])
+    )(
+        frames_in, norm1_gain, norm1_bias, norm2_gain, norm2_bias, bn_scale, bn_shift,
+        w_query, w_key, w_value, w_out, wp_blocks,
+    )
+
     return pl.pallas_call(
         lambda *refs: last_kernel(size, count, parts, *refs),
         out_shape=shape((rows, width)),
-        in_specs=[vmem, vmem, vmem] + [anywhere] * 4 + [vmem, vmem],
+        in_specs=[vmem, vmem, vmem] + [anywhere] * 4 + [vmem],
         out_specs=vmem,
         scratch_shapes=[
             pltpu.VMEM((size, rows, width), BF16),
             pltpu.VMEM((size, rows, width), BF16),
             pltpu.VMEM((size, rows, width), BF16),
             pltpu.VMEM((rows + 2 * PAD, width), F32),
-            pltpu.VMEM((size, size, width, width), BF16),
+            pltpu.VMEM((full, full), BF16),
             pltpu.VMEM((full, width), BF16),
             pltpu.VMEM((full, width), BF16),
-            pltpu.VMEM((size, width, width), BF16),
+            pltpu.VMEM((full, width), BF16),
             gather_sems(size, parts),
             gather_sems(size, parts),
             dma((4,)),
@@ -627,7 +617,10 @@
         ],
         compiler_params=params(2),
         name="convolve_project",
-    )(attended, xg, affg, wo_all, w_glu_value, w_glu_gate, wp_all, depth_kernel, norms)
+    )(
+        attended, xg, affg, wo_all.reshape(full, full), w_glu_value, w_glu_gate,
+        wp_all.reshape(full, width), depth_kernel,
+    )
 
 
 def solution(mesh):

time: 121 us -> 101 us (0.83)
  Pallas kernels: 111 us -> 99.4 us
  local copies, waits for them, and re-layouts: 9 us -> 1.78 us
    pallas_call x2 -> x1, Pallas kernels: 78.8 us -> 69.9 us  [on_device(): pl.pallas_call(lambda *refs: attend_kernel(size, count, parts, *refs), ou...]
    reshape x2 -> x0, local copies, waits for them, and re-layouts: 3 us -> none  [the longest x1 1.51 us: on_device(): wo_blocks = jnp.transpose(w_out.reshape(width, size, width), (1, 0, 2))]
    another operation x6 -> x0, local copies, waits for them, and re-layouts: 2.73 us -> none  [the longest x4 2.73 us: on_device(): jnp.stack([norm1_gain, norm1_bias, norm2_gain, norm2_bias]).astype(F32)]
    pallas_call x1, Pallas kernels: 31.8 us -> 29.5 us  [on_device(): pl.pallas_call(lambda *refs: last_kernel(size, count, parts, *refs), out_...]
    unnamed x11 -> x1, local copies, waits for them, and re-layouts: 3.26 us -> 1.78 us
where the time goes in v3:
time: 101 us
  Pallas kernels  99.4 us (98%)
  local copies, waits for them, and re-layouts  1.78 us (2%)
    pallas_call x1, Pallas kernels, on_device(): pl.pallas_call(lambda *refs: attend_kernel(size, count, parts, *refs), ou...  69.9 us
    pallas_call x1, Pallas kernels, on_device(): pl.pallas_call(lambda *refs: last_kernel(size, count, parts, *refs), out_...  29.5 us

profile of v3, /device:TPU:1, one launch (start us, length us, event | category | flops | bytes accessed | tf_op | source)
XLA Modules:
  0.0 101.2 jit_solution(15969792457120049198)
XLA Ops:
  0.0 69.9 %attend_ring.1 = (bf16[512,384]{1,0:T(8,128)(2,1)}, bf16[4,512,384]{2,1,0:T(8,128)(2,1)}, f32[4,8,384]{2,1,0:T(8,128)}, bf16[4,384,1536]{2,1,0:T(8,128)(2,1)}, bf16[4,384,384]{2,1,0:T(8,128)(2,1)}) custom-call(bf16[512,384]{1,0:T(8,128)(2,1)} %refs_0_.1, bf16[384]{0:T(512)(128)(2,1)} %refs_1_.1, bf16[384]{0:T(512)(128)(2,1)} %refs_2_.1, ...), custom_call_target="tpu_custom_call" | custom-call | tf_op jit(solution)/shard_map/attend_ring/pallas_call | solution.py:563
  69.9 29.5 %convolve_project.1 = bf16[512,384]{1,0:T(8,128)(2,1)} custom-call(bf16[512,384]{1,0:T(8,128)(2,1)} %get-tuple-element.10.refs_0_, bf16[4,512,384]{2,1,0:T(8,128)(2,1)} %get-tuple-element.11.refs_1_, f32[4,8,384]{2,1,0:T(8,128)} %get-tuple-element.12.refs_2_, bf16[1536,1536]{1,0:T(8,128)(2,1)} %bitcast.2, bf16[1536,384]{1,0:T(8,128)(2,1)} %refs_4_.3, ...), custom_call_target="tpu_custom_call" | custom-call | tf_op jit(solution)/shard_map/convolve_project/pallas_call | solution.py:599
  99.4 1.8 %copy.17 = bf16[512,384]{1,0:T(8,128)(2,1)} copy(bf16[512,384]{1,0:T(8,128)(2,1)} %convolve_project.1) | data formatting | bytes 786432

commit v4 on v3

--- a/solution.py
+++ b/solution.py
@@ -133,10 +133,10 @@
 ):
     vector_refs, refs = refs[:6], refs[6:]
     (
-        wq_hbm, wk_hbm, wv_hbm, wo_ref, wp_ref,
-        att_ref, xg_ref, affg_ref, wog_ref, wpg_ref,
+        wq_hbm, wk_hbm, wv_hbm, wo_ref,
+        att_ref, xg_ref, affg_ref, wog_ref,
         wq_ref, wk_ref, wv_ref, q_ref, kvg_ref, qm_ref, max_ref, acc_ref,
-        x_sems, aff_sems, right_sems, left_sems, wo_sems, wp_sems, load_sems, matrix_sems,
+        x_sems, aff_sems, right_sems, left_sems, wo_sems, load_sems, matrix_sems,
     ) = refs
     rows, width = x_ref.shape
     heads = width // HEAD_DIM
@@ -239,20 +239,8 @@
         target = gather.mate if step == 0 else gather.peer(step)
         remote(wo_ref, wog_ref.at[me], wo_sems.at[0, step, 0], wo_sems.at[1, step, 0], "grid", target).start()
 
-    def wp_block(index):
-        if len(wp_ref.shape) == 3:
-            return wp_ref.at[index]
-        return wp_ref.at[:, pl.ds(pl.multiple_of(index * width, LANES), width)]
-
-    def send_wp(step):
-        target = lax.rem(me + step, size)
-        return remote(wp_block(target), wpg_ref.at[me], wp_sems.at[0, step], wp_sems.at[1, step], "grid", target)
-
-    for step in range(1, size):
-        send_wp(step).start()
     loads = [
         pltpu.make_async_copy(wo_ref, wog_ref.at[me], load_sems.at[0]),
-        pltpu.make_async_copy(wp_block(me), wpg_ref.at[me], load_sems.at[1]),
     ]
     for load in loads:
         load.start()
@@ -353,10 +341,6 @@
         remote(wo_ref, wog_ref.at[me], wo_sems.at[0, step, 0], wo_sems.at[1, step, 0], "grid", target).wait_send()
     for step in range(1, gather.chips):
         gather.relay(wo_view, 0, step).wait_send()
-    for step in range(1, size):
-        send_wp(step).wait_send()
-        source = lax.rem(me + size - step, size)
-        remote(wp_block(me), wpg_ref.at[source], wp_sems.at[0, step], wp_sems.at[1, step], "grid", source).wait_recv()
     for load in loads:
         load.wait()
 
@@ -374,10 +358,10 @@
 
 
 def last_kernel(
-    size, count, parts, att_ref, xg_ref, affg_ref, wog_hbm, wgv_hbm, wgg_hbm, wpg_hbm,
+    size, count, parts, att_ref, xg_ref, affg_ref, wog_hbm, wgv_hbm, wgg_hbm, wp_hbm,
     taps_ref, out_ref,
     attg_ref, actg_ref, mid_ref, gated_ref, wo_ref, wgv_ref, wgg_ref, wp_ref,
-    att_sems, act_sems, halo_sems, load_sems,
+    att_sems, act_sems, halo_sems, load_sems, wp_sems,
 ):
     rows, width = att_ref.shape
     step_rows = rows // parts
@@ -387,16 +371,41 @@
     me = attended.me
     has_left = ctx > 0
     has_right = ctx < count - 1
+
+    def wp_block(index):
+        if len(wp_hbm.shape) == 3:
+            return wp_hbm.at[index]
+        return wp_hbm.at[:, pl.ds(pl.multiple_of(index * width, LANES), width)]
+
+    def wp_slot(index):
+        return wp_ref.at[pl.ds(pl.multiple_of(index * width, HEAD_DIM), width), :]
+
+    def send_wp(step):
+        target = lax.rem(me + step, size)
+        return remote(
+            wp_block(target), wp_slot(me), wp_sems.at[0, step], wp_sems.at[1, step], "grid", target
+        )
+
+    def take_wp(step):
+        source = lax.rem(me + size - step, size)
+        return remote(
+            wp_block(me), wp_slot(source), wp_sems.at[0, step], wp_sems.at[1, step], "grid", source
+        )
+
     loads = [
         pltpu.make_async_copy(src, dst, load_sems.at[index])
         for index, (src, dst) in enumerate(
-            ((wog_hbm, wo_ref), (wgv_hbm, wgv_ref), (wgg_hbm, wgg_ref), (wpg_hbm, wp_ref))
+            ((wog_hbm, wo_ref), (wgv_hbm, wgv_ref), (wgg_hbm, wgg_ref), (wp_block(me), wp_slot(me)))
         )
     ]
     for load in loads:
         load.start()
     barrier = pltpu.get_barrier_semaphore()
-    greeted = attended.greet(barrier)
+    greeted = size - 1
+    for step in range(1, size):
+        pl.semaphore_signal(
+            barrier, inc=1, device_id={"grid": lax.rem(me + step, size)}, device_id_type=MESH
+        )
 
     @pl.when(has_left)
     def _():
@@ -415,6 +424,8 @@
 
     for part in range(parts):
         attended.start(view(attg_ref, part), part)
+    for step in range(1, size):
+        send_wp(step).start()
 
     @pl.when(jnp.logical_not(has_left))
     def _():
@@ -446,8 +457,7 @@
             attended.forward(view(attg_ref, part + 1), part + 1)
         attended.finish(view(attg_ref, part), part)
         span = slice(part * step_rows, (part + 1) * step_rows)
-        sources = [attg_ref[index, span, :] for index in range(size)]
-        products = project(sources, wo_ref)
+        products = project([attg_ref[index, span, :] for index in range(size)], wo_ref)
         pieces = []
         for column in range(size):
             total = products[:, column * width : (column + 1) * width]
@@ -498,6 +508,8 @@
 
     sequence = inner_parts + [0] + ([parts - 1] if parts > 1 else [])
     activated.forward(view(actg_ref, sequence[0]), sequence[0])
+    for step in range(1, size):
+        take_wp(step).wait_recv()
     for order, part in enumerate(sequence):
         if order + 1 < parts:
             activated.forward(view(actg_ref, sequence[order + 1]), sequence[order + 1])
@@ -510,6 +522,8 @@
     for part in range(parts):
         attended.drain(view(attg_ref, part), part)
         activated.drain(view(actg_ref, part), part)
+    for step in range(1, size):
+        send_wp(step).wait_send()
 
     @pl.when(has_left)
     def _():
@@ -560,17 +574,16 @@
     if width % LANES:
         wp_blocks = jnp.transpose(w_proj.reshape(width, size, width), (1, 0, 2))
     weight = pltpu.VMEM((full, width), BF16)
-    attended, xg, affg, wo_all, wp_all = pl.pallas_call(
+    attended, xg, affg, wo_all = pl.pallas_call(
         lambda *refs: attend_kernel(size, count, parts, *refs),
         out_shape=(
             shape((rows, width)),
             shape((size, rows, width)),
             shape((size, 8, width), F32),
             shape((size, width, full)),
-            shape((size, width, width)),
         ),
-        in_specs=[vmem] * 7 + [anywhere] * 5,
-        out_specs=(vmem, vmem, vmem, anywhere, anywhere),
+        in_specs=[vmem] * 7 + [anywhere] * 4,
+        out_specs=(vmem, vmem, vmem, anywhere),
         scratch_shapes=[
             weight,
             weight,
@@ -585,15 +598,14 @@
             dma((2, count, parts)),
             dma((2, count, parts)),
             gather_sems(size, 1),
-            dma((2, size)),
-            dma((2,)),
+            dma((1,)),
             dma((3,)),
         ],
         compiler_params=params(1),
         name="attend_ring",
     )(
         frames_in, norm1_gain, norm1_bias, norm2_gain, norm2_bias, bn_scale, bn_shift,
-        w_query, w_key, w_value, w_out, wp_blocks,
+        w_query, w_key, w_value, w_out,
     )
 
     return pl.pallas_call(
@@ -614,12 +626,13 @@
             gather_sems(size, parts),
             dma((4,)),
             dma((4,)),
+            dma((2, size)),
         ],
         compiler_params=params(2),
         name="convolve_project",
     )(
         attended, xg, affg, wo_all.reshape(full, full), w_glu_value, w_glu_gate,
-        wp_all.reshape(full, width), depth_kernel,
+        wp_blocks, depth_kernel,
     )
 
 

time: 101 us -> 109 us (1.079)
  Pallas kernels: 99.4 us -> 107 us
    pallas_call x1, Pallas kernels: 29.5 us -> 36.9 us  [on_device(): pl.pallas_call(lambda *refs: last_kernel(size, count, parts, *refs), out_...]
where the time goes in v4:
time: 109 us; the launch traced here: 108 us
  Pallas kernels  107 us (98%)
  local copies, waits for them, and re-layouts  1.78 us (2%)
    pallas_call x1, Pallas kernels, on_device(): pl.pallas_call(lambda *refs: attend_kernel(size, count, parts, *refs), ou...  69.7 us
    pallas_call x1, Pallas kernels, on_device(): pl.pallas_call(lambda *refs: last_kernel(size, count, parts, *refs), out_...  36.9 us

profile of v4, /device:TPU:1, one launch (start us, length us, event | category | flops | bytes accessed | tf_op | source)
XLA Modules:
  0.0 108.4 jit_solution(6644779697121342752)
XLA Ops:
  0.0 69.7 %attend_ring.1 = (bf16[512,384]{1,0:T(8,128)(2,1)}, bf16[4,512,384]{2,1,0:T(8,128)(2,1)}, f32[4,8,384]{2,1,0:T(8,128)}, bf16[4,384,1536]{2,1,0:T(8,128)(2,1)}) custom-call(bf16[512,384]{1,0:T(8,128)(2,1)} %refs_0_.1, bf16[384]{0:T(512)(128)(2,1)} %refs_1_.1, bf16[384]{0:T(512)(128)(2,1)} %refs_2_.1, bf16[384]{0:T(512)(128)(2,1)} %refs_3_.1, ...), custom_call_target="tpu_custom_call" | custom-call | tf_op jit(solution)/shard_map/attend_ring/pallas_call | solution.py:577
  69.7 36.9 %convolve_project.1 = bf16[512,384]{1,0:T(8,128)(2,1)} custom-call(bf16[512,384]{1,0:T(8,128)(2,1)} %get-tuple-element.9.refs_0_, bf16[4,512,384]{2,1,0:T(8,128)(2,1)} %get-tuple-element.10.refs_1_, f32[4,8,384]{2,1,0:T(8,128)} %get-tuple-element.11.refs_2_, bf16[1536,1536]{1,0:T(8,128)(2,1)} %bitcast.1, bf16[1536,384]{1,0:T(8,128)(2,1)} %refs_4_.3, ...), custom_call_target="tpu_custom_call" | custom-call | tf_op jit(solution)/shard_map/convolve_project/pallas_call | solution.py:611
  106.6 1.8 %copy.17 = bf16[512,384]{1,0:T(8,128)(2,1)} copy(bf16[512,384]{1,0:T(8,128)(2,1)} %convolve_project.1) | data formatting | bytes 786432
